TPU v7x, 32 devices: a whole 2x2x4 slice. The times are simulated.
32 devices in a mesh: section: 4 (over y, x), seq: 8 (over z, core).
Axes of the slice: x: 2, y: 2, z: 4, core: 2. Of those that a mesh axis runs over, the one named last changes fastest.
Arguments:
- inflow: bfloat16 [4, 512, 4096], P('section', 'seq'), may hold values from -6 to 6
- fresh: bfloat16 [1, 512, 4096], P(None, 'seq'), may hold values from -6 to 6
- proj_weight: bfloat16 [4, 4096, 640], P('section'), may hold values from -0.09375 to 0.09375
- xz_weight: bfloat16 [4, 4096, 2, 4096], P('section', None, None, 'seq'), may hold values from -0.09375 to 0.09375
- conv_weight: float32 [4, 4, 4608], P('section'), may hold values from -3 to 3
- conv_bias: float32 [4, 4608], P('section'), may hold values from -3 to 3
- step_bias: float32 [4, 128], P('section'), may hold values from -3 to 0
- decay_log: float32 [4, 128], P('section'), may hold values from -7 to -1
- skip_weight: float32 [4, 128], P('section'), may hold values from 0.5 to 1.5
- norm_gain: float32 [4, 4096], P('section'), may hold values from 0.5 to 1.5
- out_weight: bfloat16 [4, 4096, 4096], P('section', 'seq'), may hold values from -0.09375 to 0.09375
Outputs:
- section_outputs: float32 [4, 2, 512, 4096], P('section', None, 'seq')
All inputs are finite; a program needn't handle non-finite values.
Results may differ from a plain program's by a relative error of at most 0.014.
Values may be sent and summed in bfloat16 or wider, within the bound.
No kernel may reach another device: no remote copies, remote signals or barrier semaphores. Data moves between devices by JAX's collectives and lax.ppermute only.
A program may use at most 128 MiB of HBM per device.

v0:
```python
import functools

import jax
import jax.numpy as jnp
from jax import lax
from jax.experimental import pallas as pl
from jax.experimental.pallas import tpu as pltpu
from jax.sharding import PartitionSpec as P


HEADS = 128
HEAD_DIM = 32
STATE = 64
GROUPS = 4
CONV = 4
BLOCK = 128
LANES = 128
PIECES = 2
QUAD = LANES // HEAD_DIM


bf16 = jnp.bfloat16
f32 = jnp.float32


def swapped(value, bit):
    count = lax.axis_size("seq")
    return lax.ppermute(value, "seq", [(i, i ^ bit) for i in range(count)])


def chip_ring(value):
    count = lax.axis_size("seq")
    return lax.ppermute(value, "seq", [(i, (i + 2) % count) for i in range(count)])


def next_section(value, chips_on):
    sections, count = lax.axis_size("section"), lax.axis_size("seq")
    pairs = [
        (s * count + i, (s + 1) % sections * count + (i + 2 * chips_on) % count)
        for s in range(sections)
        for i in range(count)
    ]
    return lax.ppermute(value, ("section", "seq"), pairs)


IN_VMEM = pl.BlockSpec(memory_space=pltpu.VMEM)
IN_SMEM = pl.BlockSpec(memory_space=pltpu.SMEM)
PARAMS = pltpu.CompilerParams(vmem_limit_bytes=16 * 1024 * 1024)


def after(values, *others):
    return lax.optimization_barrier((values, others))[0]


def chip_at(where, steps, chips):
    return lax.rem(where[0] + (chips - steps), chips)


def project_kernel(where, *refs, steps, chips):
    xs, refs = refs[: 2 * PIECES], refs[2 * PIECES :]
    weights, outs = refs[:2], refs[-2:]
    core = where[1]
    tokens, depth = xs[0].shape
    start = chip_at(where, steps, chips) * (2 * tokens)
    mine = pl.ds(pl.multiple_of(start + core * tokens, tokens), tokens)
    other = pl.ds(pl.multiple_of(start + (1 - core) * tokens, tokens), tokens)
    tall = [
        jnp.concatenate([xs[i][...], xs[PIECES + i][...]], axis=0) for i in range(PIECES)
    ]
    for weight, out in zip(weights, outs):
        total = None
        for i, x in enumerate(tall):
            part = jnp.dot(
                x, weight[i * depth : (i + 1) * depth, :], preferred_element_type=f32
            )
            total = part if total is None else total + part
        total = total.astype(bf16)
        out[mine, :] = total[:tokens]
        out[other, :] = total[tokens:]


def project(where, steps, chips, xs, weights, length, buffers):
    args = [where, *xs, *weights]
    in_specs = [IN_SMEM] + [IN_VMEM] * (len(args) - 1)
    aliases = {}
    if buffers is not None:
        aliases = {len(args): 0, len(args) + 1: 1}
        args += list(buffers)
        in_specs += [IN_VMEM] * 2
    width = weights[0].shape[0]
    columns = sum(weight.shape[1] for weight in weights)
    return pl.pallas_call(
        functools.partial(project_kernel, steps=steps, chips=chips),
        in_specs=in_specs,
        out_specs=[IN_VMEM] * 2,
        out_shape=[jax.ShapeDtypeStruct((length, weight.shape[1]), bf16) for weight in weights],
        input_output_aliases=aliases,
        compiler_params=PARAMS,
        cost_estimate=pl.CostEstimate(
            flops=2 * (length // chips) * width * columns,
            bytes_accessed=2 * width * columns,
            transcendentals=0,
        ),
        name="project",
    )(*args)


def ready_kernel(where, xz_ref, p_ref, out):
    del xz_ref, p_ref
    out[0] = where[0]
    out[1] = where[1]


def ready(where, xz_local, p_local):
    anywhere = pl.BlockSpec(memory_space=pl.ANY)
    return pl.pallas_call(
        ready_kernel,
        in_specs=[IN_SMEM, anywhere, anywhere],
        out_specs=IN_SMEM,
        out_shape=jax.ShapeDtypeStruct(where.shape, where.dtype),
        compiler_params=PARAMS,
        name="ready",
    )(where, xz_local, p_local)


def spread_of(chans):
    return (
        lax.broadcasted_iota(jnp.int32, (LANES, chans), 0)
        == lax.broadcasted_iota(jnp.int32, (LANES, chans), 1) // HEAD_DIM
    )


def tables_kernel(
    where, conv_w, conv_b, step_b, decay, skip_w, norm_g,
    taps, offset, bias, rate, skip, gain,
):
    chans = gain.shape[1]
    heads = chans // HEAD_DIM
    member = where[0] * 2 + where[1]
    first = member * heads
    group = first // (HEADS // GROUPS)
    odd = lax.rem(group, 2) == 1
    own = pl.ds(pl.multiple_of(member * chans, LANES), chans)
    inner = HEADS * HEAD_DIM
    for table, out in ((conv_w, taps), (conv_b, offset)):
        out[:, :chans] = table[:, own]
        b_at = pl.multiple_of(inner + group // 2 * LANES, LANES)
        c_at = pl.multiple_of(inner + GROUPS * STATE + group // 2 * LANES, LANES)
        count = table.shape[0]
        rows = []
        for k in range(count):
            b = jnp.broadcast_to(table[k : k + 1, pl.ds(b_at, LANES)], (8, LANES))
            c = jnp.broadcast_to(table[k : k + 1, pl.ds(c_at, LANES)], (8, LANES))
            b = jnp.where(odd, pltpu.roll(b, STATE, 1), b)
            c = jnp.where(odd, c, pltpu.roll(c, STATE, 1))
            lane = lax.broadcasted_iota(jnp.int32, (8, LANES), 1)
            rows.append(jnp.where(lane < STATE, b, c)[0:1])
        for k in range(count):
            out[k : k + 1, chans:] = rows[k]
    back = lax.rem(HEADS - first, HEADS)

    def own_heads(table):
        return pltpu.roll(jnp.broadcast_to(table[...], (8, LANES)), back, 1)

    bias[...] = own_heads(step_b)[0:1]
    rate[...] = -jnp.exp(own_heads(decay)[0:1])
    skip[...] = jnp.dot(
        own_heads(skip_w),
        spread_of(chans).astype(f32),
        precision=lax.Precision.HIGHEST,
        preferred_element_type=f32,
    )[0:1]
    gain[...] = norm_g[:, own]


def tables_of(where, params, chans):
    shapes = (
        (CONV, chans + 2 * STATE), (1, chans + 2 * STATE), (1, LANES), (1, LANES), (1, chans),
        (1, chans),
    )
    return pl.pallas_call(
        tables_kernel,
        in_specs=[IN_SMEM] + [IN_VMEM] * len(params),
        out_specs=[IN_VMEM] * len(shapes),
        out_shape=[jax.ShapeDtypeStruct(shape, f32) for shape in shapes],
        compiler_params=PARAMS,
        name="tables",
    )(where, *params)


def silu(value):
    return value / (1.0 + jnp.exp(-value))


def split_terms(value, terms):
    parts = []
    for _ in range(terms - 1):
        parts.append(value.astype(bf16))
        value = value - parts[-1].astype(f32)
    return parts + [value.astype(bf16)]


def mix_kernel(
    where, xz_ref, p_ref, taps_ref, offset_ref, bias_ref, rate_ref, skip_ref, gain_ref,
    mine_ref, theirs_ref, mine_squares, theirs_squares,
    padded_ref, state_ref, gated_ref, squares_ref,
):
    chans = mine_ref.shape[1]
    heads = chans // HEAD_DIM
    lead = 8
    rows = pl.ds(pl.multiple_of(pl.program_id(0) * BLOCK, BLOCK), BLOCK)

    @pl.when(pl.program_id(0) == 0)
    def _():
        padded_ref[0:lead, :] = jnp.zeros((lead, padded_ref.shape[1]), f32)
        state_ref[...] = jnp.zeros_like(state_ref)

    padded_ref[lead : lead + BLOCK, 0:chans] = xz_ref[rows, chans:].astype(f32)
    padded_ref[lead : lead + BLOCK, chans:] = p_ref[rows, 0 : 2 * STATE].astype(f32)
    total = offset_ref[0:1, :]
    for k in range(CONV):
        start = lead - (CONV - 1) + k
        total = total + taps_ref[k : k + 1, :] * padded_ref[start : start + BLOCK, :]
    padded_ref[0:lead, :] = padded_ref[BLOCK : BLOCK + lead, :]
    convolved = silu(total).astype(bf16)
    x = convolved[:, :chans]
    bc = convolved[:, chans:]
    b = bc[:, :STATE]
    c = bc[:, STATE:]

    step = jax.nn.softplus(p_ref[rows, 2 * STATE :].astype(f32) + bias_ref[0:1, :])
    decay = rate_ref[0:1, :] * step
    row = lax.broadcasted_iota(jnp.int32, (BLOCK, BLOCK), 0)
    col = lax.broadcasted_iota(jnp.int32, (BLOCK, BLOCK), 1)
    lower = row >= col
    terms = split_terms(decay, 3)
    cumulus = jnp.dot(
        jnp.concatenate([lower.astype(bf16)] * len(terms), axis=1),
        jnp.concatenate(terms, axis=0),
        preferred_element_type=f32,
    )
    block_total = cumulus[BLOCK - 1 : BLOCK, :]
    cumulus_t = cumulus.T
    step_t = step.T
    scores = lax.dot_general(c, b, (((1,), (1,)), ((), ())), preferred_element_type=f32)
    spread = spread_of(chans).astype(bf16)
    spread = jnp.concatenate([spread, spread], axis=0)

    def per_channel(table):
        return jnp.dot(
            jnp.concatenate(split_terms(table, 2), axis=1), spread, preferred_element_type=f32
        )

    grown = per_channel(jnp.exp(cumulus))
    kept = per_channel(jnp.exp(block_total - cumulus) * step)
    x_wide = x.astype(f32)
    weighted = (x_wide * kept).astype(bf16)
    entering = state_ref[...].astype(bf16)
    carried = jnp.dot(c, entering, preferred_element_type=f32) * grown
    block_state = lax.dot_general(
        b, weighted, (((0,), (0,)), ((), ())), preferred_element_type=f32
    )
    state_ref[...] = grown[BLOCK - 1 : BLOCK, :] * state_ref[...] + block_state

    lane_head = lax.broadcasted_iota(jnp.int32, (BLOCK, LANES), 1) // HEAD_DIM
    squares = jnp.zeros((BLOCK, 1), f32)
    for quad in range(heads // QUAD):
        lanes = slice(quad * LANES, (quad + 1) * LANES)
        x_quad = x[:, lanes]
        left, right = [], []
        for j in range(QUAD):
            h = quad * QUAD + j
            gap = jnp.where(lower, cumulus[:, h : h + 1] - cumulus_t[h : h + 1, :], -1e30)
            left.append((scores * jnp.exp(gap) * step_t[h : h + 1, :]).astype(bf16))
            right.append(jnp.where(lane_head == j, x_quad, jnp.zeros_like(x_quad)))
        diagonal = jnp.dot(
            jnp.concatenate(left, axis=1),
            jnp.concatenate(right, axis=0),
            preferred_element_type=f32,
        )
        mixed = diagonal + carried[:, lanes] + skip_ref[0:1, lanes] * x_wide[:, lanes]
        gated = mixed * silu(xz_ref[rows, lanes].astype(f32))
        squares = squares + jnp.sum(gated * gated, axis=1, keepdims=True)
        gated_ref[:, lanes] = (gated * gain_ref[0:1, lanes]).astype(bf16)
    squares_ref[...] = jnp.broadcast_to(squares, (BLOCK, LANES))
    part = BLOCK // 2
    core = where[1]
    to = pl.ds(pl.multiple_of(pl.program_id(0) * part, part), part)
    near = pl.ds(pl.multiple_of(core * part, part), part)
    far = pl.ds(pl.multiple_of((1 - core) * part, part), part)
    mine_ref[to, :] = gated_ref[near, :]
    theirs_ref[to, :] = gated_ref[far, :]
    mine_squares[to, :] = squares_ref[near, :]
    theirs_squares[to, :] = squares_ref[far, :]


def mix(where, xz, p, tables):
    length, both = xz.shape
    chans = both // 2
    n_p = p.shape[1]
    return pl.pallas_call(
        mix_kernel,
        grid=(length // BLOCK,),
        in_specs=[IN_SMEM] + [IN_VMEM] * (2 + len(tables)),
        out_specs=[IN_VMEM] * 4,
        compiler_params=PARAMS,
        out_shape=[jax.ShapeDtypeStruct((length // 2, chans), bf16)] * 2
        + [jax.ShapeDtypeStruct((length // 2, LANES), f32)] * 2,
        scratch_shapes=[
            pltpu.VMEM((BLOCK + 8, chans + 2 * STATE), f32),
            pltpu.VMEM((STATE, chans), f32),
            pltpu.VMEM((BLOCK, chans), bf16),
            pltpu.VMEM((BLOCK, LANES), f32),
        ],
        cost_estimate=pl.CostEstimate(
            flops=2 * length * chans * BLOCK * 8,
            bytes_accessed=2 * length * (both + chans + n_p),
            transcendentals=length * chans * 4,
        ),
        name="mix",
    )(where, xz, p, *tables)


def out_kernel(where, g_mine, g_other, w_mine, w_other, *refs, steps, chips, first, count, scale):
    squares, outs = refs[:-count], refs[-count:]
    rows, tile = outs[0].shape
    at = pl.ds(pl.multiple_of(chip_at(where, steps, chips) * rows, rows), rows)
    total = squares[0][at, 0:1]
    for more in squares[1:]:
        total = total + more[at, 0:1]
    rate = lax.rsqrt(total * scale + 1e-05)
    for i, out in enumerate(outs):
        cols = slice((first + i) * tile, (first + i + 1) * tile)
        part = jnp.dot(g_mine[at, :], w_mine[:, cols], preferred_element_type=f32)
        part = part + jnp.dot(g_other[at, :], w_other[:, cols], preferred_element_type=f32)
        out[...] = (part * rate).astype(out.dtype)


def out_project(where, steps, chips, gated, weights, squares, pieces, dtype):
    chans, cols = weights[0].shape
    rows = gated[0].shape[0] // chips
    first, count = pieces
    args = [where, *gated, *weights, *squares]
    return pl.pallas_call(
        functools.partial(
            out_kernel,
            steps=steps,
            chips=chips,
            first=first,
            count=count,
            scale=GROUPS / (HEADS * HEAD_DIM),
        ),
        in_specs=[IN_SMEM] + [IN_VMEM] * (len(args) - 1),
        out_specs=[IN_VMEM] * count,
        out_shape=[jax.ShapeDtypeStruct((rows, cols // PIECES), dtype)] * count,
        compiler_params=PARAMS,
        cost_estimate=pl.CostEstimate(
            flops=4 * rows * chans * cols * count // PIECES,
            bytes_accessed=4 * chans * cols * count // PIECES,
            transcendentals=0,
        ),
        name="out_project",
    )(*args)


def on_device(
    inflow,
    fresh,
    proj_weight,
    xz_weight,
    conv_weight,
    conv_bias,
    step_bias,
    decay_log,
    skip_weight,
    norm_gain,
    out_weight,
):
    members = lax.axis_size("seq")
    sections = lax.axis_size("section")
    position = lax.axis_index("section")
    member = lax.axis_index("seq")
    chips = members // 2
    tokens, width = inflow.shape[1], inflow.shape[2]
    assert 2 * tokens == BLOCK
    length = tokens * members
    piece = width // PIECES
    heads_dev = HEADS // members
    chan_dev = heads_dev * HEAD_DIM
    bc_width = GROUPS * STATE
    group_members = members // GROUPS
    head_start = member * heads_dev
    group_index = head_start // (HEADS // GROUPS)
    where = jnp.stack([member // 2, member % 2]).astype(jnp.int32)

    def in_pieces(shard):
        return [shard[:, i * piece : (i + 1) * piece] for i in range(PIECES)]

    entering = in_pieces(inflow[0])
    arriving = [chip_ring(x) for x in entering]

    xz_local = xz_weight[0].reshape(width, 2 * chan_dev)
    column = lax.broadcasted_iota(jnp.int32, (proj_weight.shape[2], 2 * LANES), 1)
    source = jnp.where(
        column < STATE,
        group_index * STATE + column,
        jnp.where(
            column < 2 * STATE,
            bc_width + group_index * STATE + column - STATE,
            2 * bc_width + head_start + column - 2 * STATE,
        ),
    )
    chosen = (lax.broadcasted_iota(jnp.int32, column.shape, 0) == source) & (
        column < 2 * STATE + heads_dev
    )
    p_local = jnp.dot(
        proj_weight[0], chosen.astype(bf16), preferred_element_type=f32
    ).astype(bf16)
    where_ready = ready(where, xz_local, p_local)
    tables = tables_of(
        where, (conv_weight[0], conv_bias, step_bias, decay_log, skip_weight, norm_gain), chan_dev
    )
    out_weights = (out_weight[0], swapped(out_weight[0], 1))

    def layer(held, arriving):
        buffers = None
        for step in range(chips):
            if step == 1:
                held = arriving
            elif step > 1:
                held = [chip_ring(x) for x in held]
            other = [swapped(part, 1) for part in held]
            buffers = project(
                where_ready, step, chips, held + other, (xz_local, p_local), length, buffers
            )
        near, far, near_squares, far_squares = mix(where, *buffers, tables)
        gated = (near, swapped(far, 1))
        squares = []
        for mask in range(0, group_members, 2):
            squares.append(swapped(near_squares, mask) if mask else near_squares)
            squares.append(swapped(far_squares, mask ^ 1))
        running = None
        for step in range(1, chips + 1):
            calls = [(i, 1) for i in range(PIECES)] if step == 1 else [(0, PIECES)]
            parts = []
            for call in calls:
                parts += out_project(
                    where, step, chips, gated, out_weights, squares, call,
                    bf16 if step == 1 else f32,
                )
            if running is not None:
                parts = [part + came.astype(f32) for part, came in zip(parts, running)]
            if step < chips:
                running = [chip_ring(part.astype(bf16)) for part in parts]
        return parts

    first = layer(entering, arriving)
    leaving = [
        jnp.where(position == sections - 1, new, part.astype(bf16))
        for new, part in zip(in_pieces(fresh[0]), first)
    ]
    ahead = [next_section(x, 1) for x in leaving]
    level = [next_section(x, 0) for x in after(leaving, ahead)]
    second = layer(level, ahead)
    return jnp.stack([jnp.concatenate(first, axis=1), jnp.concatenate(second, axis=1)])[None]


def solution(mesh):
    placed = (
        P("section", "seq", None),
        P(None, "seq", None),
        P("section", None, None),
        P("section", None, None, "seq"),
        P("section", None, None),
        P("section", None),
        P("section", None),
        P("section", None),
        P("section", None),
        P("section", None),
        P("section", "seq", None),
    )

    return jax.shard_map(
        on_device,
        mesh=mesh,
        in_specs=placed,
        out_specs=P("section", None, "seq", None),
        check_vma=False,
    )
```

profile of v0, /device:TPU:0, one launch (start us, length us, event | category | flops | bytes accessed | tf_op | source)
XLA Modules:
  0.0 226.5 jit_solution(1832731076009774310)
XLA Ops:
  6.3 7.1 %collective-permute-done.refs_0_ = bf16[64,2048]{1,0:T(8,128)(2,1)S(1)} collective-permute-done((bf16[64,2048]{1,0:T(8,128)(2,1)S(1)}, bf16[64,2048]{1,0:T(8,128)(2,1)S(1)}, u32[]{:S(2)}, u32[]{:S(2)}) %collective-permute-start) | collective-permute-done | bytes 262176 | tf_op jit(solution)/shard_map/ppermute | solution.py:33
  13.4 5.6 %collective-permute-done.3.refs_1_ = bf16[64,2048]{1,0:T(8,128)(2,1)S(1)} collective-permute-done((bf16[64,2048]{1,0:T(8,128)(2,1)S(1)}, bf16[64,2048]{1,0:T(8,128)(2,1)S(1)}, u32[]{:S(2)}, u32[]{:S(2)}) %collective-permute-start.3) | collective-permute-done | bytes 262176 | tf_op jit(solution)/shard_map/ppermute | solution.py:33
  20.3 4.4 %collective-permute-done.1.refs_0_ = bf16[64,2048]{1,0:T(8,128)(2,1)} collective-permute-done((bf16[64,2048]{1,0:T(8,128)(2,1)S(1)}, bf16[64,2048]{1,0:T(8,128)(2,1)}, u32[]{:S(2)}, u32[]{:S(2)}) %collective-permute-start.1) | collective-permute-done | bytes 262176 | tf_op jit(solution)/shard_map/ppermute | solution.py:33
  24.7 5.6 %collective-permute-done.4.refs_1_ = bf16[64,2048]{1,0:T(8,128)(2,1)} collective-permute-done((bf16[64,2048]{1,0:T(8,128)(2,1)S(1)}, bf16[64,2048]{1,0:T(8,128)(2,1)}, u32[]{:S(2)}, u32[]{:S(2)}) %collective-permute-start.4) | collective-permute-done | bytes 262176 | tf_op jit(solution)/shard_map/ppermute | solution.py:33
  30.3 4.4 %fusion.5.p_ref.refs_5_ = bf16[4096,256]{1,0:T(8,128)(2,1)S(1)} fusion(bf16[1,4096,640]{2,1,0:T(8,128)(2,1)} %param.13, s32[256]{0:T(256)S(1)} %get-tuple-element.103, s32[256]{0:T(256)S(1)} %get-tuple-element.104, s32[256]{0:T(256)S(1)} %iota_add_fusion, pred[256]{0:T(512)(128)(4,1)S(1)} %get-tuple-element.101, pred[256]{0:T(512)(128)(4,1)S(1)} %get-tuple-element.102, ...), kind=kOutput, calls=%fused_computation.3 | convolution fusion | flops 1343881216 | bytes 7343872 | tf_op jit(solution)/shard_map/dot_general | solution.py:416
  35.4 9.4 %copy.26 = bf16[512,8,2,512]{3,1,2,0:T(8,128)(2,1)} copy(bf16[512,8,2,512]{3,2,1,0:T(2,128)(2,1)} %bitcast.45) | data formatting | bytes 16777216
  61.8 6.2 %mix.2 = (bf16[256,512]{1,0:T(8,128)(2,1)S(1)}, bf16[256,512]{1,0:T(8,128)(2,1)S(1)}, f32[256,128]{1,0:T(8,128)S(1)}, f32[256,128]{1,0:T(8,128)S(1)}) custom-call(s32[2]{0:T(128)S(1)} %pad_add_fusion.where, bf16[512,1024]{1,0:T(8,128)(2,1)S(1)} %get-tuple-element.55.xz_ref, bf16[512,256]{1,0:T(8,128)(2,1)S(1)} %get-tuple-element.56.p_ref, ...), custom_call_target="tpu_custom_call" | custom-call | flops 536870912 | bytes 1835008 | tf_op jit(solution)/shard_map/mix/pallas_call | solution.py:301
  82.9 3.8 %out_project.11 = (f32[64,2048]{1,0:T(8,128)S(1)}, f32[64,2048]{1,0:T(8,128)S(1)}) custom-call(s32[2]{0:T(128)S(1)} %pad_add_fusion.where, bf16[256,512]{1,0:T(8,128)(2,1)S(1)} %get-tuple-element.63.g_mine, bf16[256,512]{1,0:T(8,128)(2,1)S(1)} %collective-permute-done.14.g_other, bf16[512,4096]{1,0:T(8,128)(2,1)S(1)} %bitcast.37, ...), custom_call_target="tpu_custom_call" | custom-call | flops 536870912 | bytes 8388608 | tf_op jit(solution)/shard_map/out_project/pallas_call | solution.py:344
  89.1 8.7 %collective-permute-done.18 = bf16[64,2048]{1,0:T(8,128)(2,1)S(1)} collective-permute-done((bf16[64,2048]{1,0:T(8,128)(2,1)S(1)}, bf16[64,2048]{1,0:T(8,128)(2,1)S(1)}, u32[]{:S(2)}, u32[]{:S(2)}) %collective-permute-start.18) | collective-permute-done | bytes 262176 | tf_op jit(solution)/shard_map/ppermute | solution.py:33
  97.9 5.5 %collective-permute-done.21 = bf16[64,2048]{1,0:T(8,128)(2,1)S(1)} collective-permute-done((bf16[64,2048]{1,0:T(8,128)(2,1)S(1)}, bf16[64,2048]{1,0:T(8,128)(2,1)S(1)}, u32[]{:S(2)}, u32[]{:S(2)}) %collective-permute-start.21) | collective-permute-done | bytes 262176 | tf_op jit(solution)/shard_map/ppermute | solution.py:33
  105.8 3.8 %out_project.10 = (f32[64,2048]{1,0:T(8,128)S(1)}, f32[64,2048]{1,0:T(8,128)S(1)}) custom-call(s32[2]{0:T(128)S(1)} %pad_add_fusion.where, bf16[256,512]{1,0:T(8,128)(2,1)S(1)} %get-tuple-element.63.g_mine, bf16[256,512]{1,0:T(8,128)(2,1)S(1)} %collective-permute-done.14.g_other, bf16[512,4096]{1,0:T(8,128)(2,1)S(1)} %bitcast.38, ...), custom_call_target="tpu_custom_call" | custom-call | flops 536870912 | bytes 8388608 | tf_op jit(solution)/shard_map/out_project/pallas_call | solution.py:344
  117.0 10.4 %collective-permute-done.23.refs_0_ = bf16[64,2048]{1,0:T(8,128)(2,1)S(1)} collective-permute-done((bf16[64,2048]{1,0:T(8,128)(2,1)S(1)}, bf16[64,2048]{1,0:T(8,128)(2,1)S(1)}, u32[]{:S(2)}, u32[]{:S(2)}) %collective-permute-start.23) | collective-permute-done | bytes 262176 | tf_op jit(solution)/shard_map/ppermute | solution.py:43
  133.8 6.8 %collective-permute-done.35.refs_0_ = bf16[64,2048]{1,0:T(8,128)(2,1)S(1)} collective-permute-done((bf16[64,2048]{1,0:T(8,128)(2,1)S(1)}, bf16[64,2048]{1,0:T(8,128)(2,1)S(1)}, u32[]{:S(2)}, u32[]{:S(2)}) %collective-permute-start.35) | collective-permute-done | bytes 262176 | tf_op jit(solution)/shard_map/ppermute | solution.py:43
  147.3 7.6 %collective-permute-done.25.refs_0_ = bf16[64,2048]{1,0:T(8,128)(2,1)S(1)} collective-permute-done((bf16[64,2048]{1,0:T(8,128)(2,1)S(1)}, bf16[64,2048]{1,0:T(8,128)(2,1)S(1)}, u32[]{:S(2)}, u32[]{:S(2)}) %collective-permute-start.25) | collective-permute-done | bytes 262176 | tf_op jit(solution)/shard_map/ppermute | solution.py:33
  154.9 4.6 %collective-permute-done.28.refs_1_ = bf16[64,2048]{1,0:T(8,128)(2,1)S(1)} collective-permute-done((bf16[64,2048]{1,0:T(8,128)(2,1)S(1)}, bf16[64,2048]{1,0:T(8,128)(2,1)S(1)}, u32[]{:S(2)}, u32[]{:S(2)}) %collective-permute-start.28) | collective-permute-done | bytes 262176 | tf_op jit(solution)/shard_map/ppermute | solution.py:33
  171.6 6.0 %mix.3 = (bf16[256,512]{1,0:T(8,128)(2,1)S(1)}, bf16[256,512]{1,0:T(8,128)(2,1)S(1)}, f32[256,128]{1,0:T(8,128)S(1)}, f32[256,128]{1,0:T(8,128)S(1)}) custom-call(s32[2]{0:T(128)S(1)} %pad_add_fusion.where, bf16[512,1024]{1,0:T(8,128)(2,1)S(1)} %get-tuple-element.81.xz_ref, bf16[512,256]{1,0:T(8,128)(2,1)S(1)} %get-tuple-element.82.p_ref, ...), custom_call_target="tpu_custom_call" | custom-call | flops 536870912 | bytes 1835008 | tf_op jit(solution)/shard_map/mix/pallas_call | solution.py:301
  186.2 3.8 %out_project.17 = (f32[64,2048]{1,0:T(8,128)S(1)}, f32[64,2048]{1,0:T(8,128)S(1)}) custom-call(s32[2]{0:T(128)S(1)} %pad_add_fusion.where, bf16[256,512]{1,0:T(8,128)(2,1)S(1)} %get-tuple-element.83.g_mine, bf16[256,512]{1,0:T(8,128)(2,1)S(1)} %collective-permute-done.39.g_other, bf16[512,4096]{1,0:T(8,128)(2,1)S(1)} %bitcast.41, ...), custom_call_target="tpu_custom_call" | custom-call | flops 536870912 | bytes 8388608 | tf_op jit(solution)/shard_map/out_project/pallas_call | solution.py:344
  190.0 3.8 %out_project.16 = (f32[64,2048]{1,0:T(8,128)S(1)}, f32[64,2048]{1,0:T(8,128)S(1)}) custom-call(s32[2]{0:T(128)S(1)} %pad_add_fusion.where, bf16[256,512]{1,0:T(8,128)(2,1)S(1)} %get-tuple-element.83.g_mine, bf16[256,512]{1,0:T(8,128)(2,1)S(1)} %collective-permute-done.39.g_other, bf16[512,4096]{1,0:T(8,128)(2,1)S(1)} %bitcast.42, ...), custom_call_target="tpu_custom_call" | custom-call | flops 536870912 | bytes 8388608 | tf_op jit(solution)/shard_map/out_project/pallas_call | solution.py:344
  193.7 3.8 %out_project.15 = (f32[64,2048]{1,0:T(8,128)S(1)}, f32[64,2048]{1,0:T(8,128)S(1)}) custom-call(s32[2]{0:T(128)S(1)} %pad_add_fusion.where, bf16[256,512]{1,0:T(8,128)(2,1)S(1)} %get-tuple-element.83.g_mine, bf16[256,512]{1,0:T(8,128)(2,1)S(1)} %collective-permute-done.39.g_other, bf16[512,4096]{1,0:T(8,128)(2,1)S(1)} %bitcast.43, ...), custom_call_target="tpu_custom_call" | custom-call | flops 536870912 | bytes 8388608 | tf_op jit(solution)/shard_map/out_project/pallas_call | solution.py:344
  198.7 3.9 %collective-permute-start.45 = (bf16[64,2048]{1,0:T(8,128)(2,1)S(1)}, bf16[64,2048]{1,0:T(8,128)(2,1)S(1)}, u32[]{:S(2)}, u32[]{:S(2)}) collective-permute-start(bf16[64,2048]{1,0:T(8,128)(2,1)S(1)} %add_convert_fusion.1), channel_id=1, source_target_pairs={{0,2},{1,3},{2,4},{3,5},{4,6},{5,7},{6,0},{7,1},{8,10},{9,11},{10,... | collective-permute-start | bytes 786440 | tf_op jit(solution)/shard_map/ppermute | solution.py:33
  202.7 6.0 %collective-permute-done.42 = bf16[64,2048]{1,0:T(8,128)(2,1)S(1)} collective-permute-done((bf16[64,2048]{1,0:T(8,128)(2,1)S(1)}, bf16[64,2048]{1,0:T(8,128)(2,1)S(1)}, u32[]{:S(2)}, u32[]{:S(2)}) %collective-permute-start.42) | collective-permute-done | bytes 262176 | tf_op jit(solution)/shard_map/ppermute | solution.py:33
  209.4 4.9 %collective-permute-done.45 = bf16[64,2048]{1,0:T(8,128)(2,1)S(1)} collective-permute-done((bf16[64,2048]{1,0:T(8,128)(2,1)S(1)}, bf16[64,2048]{1,0:T(8,128)(2,1)S(1)}, u32[]{:S(2)}, u32[]{:S(2)}) %collective-permute-start.45) | collective-permute-done | bytes 262176 | tf_op jit(solution)/shard_map/ppermute | solution.py:33
  215.0 4.9 %collective-permute-done.43 = bf16[64,2048]{1,0:T(8,128)(2,1)S(1)} collective-permute-done((bf16[64,2048]{1,0:T(8,128)(2,1)S(1)}, bf16[64,2048]{1,0:T(8,128)(2,1)S(1)}, u32[]{:S(2)}, u32[]{:S(2)}) %collective-permute-start.43) | collective-permute-done | bytes 262176 | tf_op jit(solution)/shard_map/ppermute | solution.py:33
  219.9 5.0 %collective-permute-done.46 = bf16[64,2048]{1,0:T(8,128)(2,1)S(1)} collective-permute-done((bf16[64,2048]{1,0:T(8,128)(2,1)S(1)}, bf16[64,2048]{1,0:T(8,128)(2,1)S(1)}, u32[]{:S(2)}, u32[]{:S(2)}) %collective-permute-start.46) | collective-permute-done | bytes 262176 | tf_op jit(solution)/shard_map/ppermute | solution.py:33
  (144 shorter events, 90.0 us)
Async XLA Ops:
  0.0 69.8 %collective-permute-start.15 = (bf16[512,4096]{1,0:T(8,128)(2,1)}, bf16[512,4096]{1,0:T(8,128)(2,1)}, u32[]{:S(2)}, u32[]{:S(2)}) collective-permute-start(bf16[512,4096]{1,0:T(8,128)(2,1)} %bitcast.33), channel_id=1, source_target_pairs={{0,1},{1,0},{2,3},{3,2},{4,5},{5,4},{6,7},{7,6},{8,9},{9,8},{10,11... | collective-permute-start | bytes 12582920 | tf_op jit(solution)/shard_map/ppermute | solution.py:28
  4.2 14.8 %collective-permute-start.3 = (bf16[64,2048]{1,0:T(8,128)(2,1)S(1)}, bf16[64,2048]{1,0:T(8,128)(2,1)S(1)}, u32[]{:S(2)}, u32[]{:S(2)}) collective-permute-start(bf16[64,2048]{1,0:T(8,128)(2,1)S(1)} %get-tuple-element.99.refs_1_), channel_id=1, source_target_pairs={{0,2},{1,3},{2,4},{3,5},{4,6},{5,7},{6,0},{7,1},{8,10},{9,11},{10,... | collective-permute-start | bytes 786440 | tf_op jit(solution)/shard_map/ppermute | solution.py:33
  5.8 13.3 %collective-permute-start.12 = (bf16[64,2048]{1,0:T(8,128)(2,1)S(1)}, bf16[64,2048]{1,0:T(8,128)(2,1)S(1)}, u32[]{:S(2)}, u32[]{:S(2)}) collective-permute-start(bf16[64,2048]{1,0:T(8,128)(2,1)S(1)} %get-tuple-element.100.refs_0_), channel_id=1, source_target_pairs={{0,1},{1,0},{2,3},{3,2},{4,5},{5,4},{6,7},{7,6},{8,9},{9,8},{10,11... | collective-permute-start | bytes 786440 | tf_op jit(solution)/shard_map/ppermute | solution.py:28
  5.8 13.3 %collective-permute-start.13 = (bf16[64,2048]{1,0:T(8,128)(2,1)S(1)}, bf16[64,2048]{1,0:T(8,128)(2,1)S(1)}, u32[]{:S(2)}, u32[]{:S(2)}) collective-permute-start(bf16[64,2048]{1,0:T(8,128)(2,1)S(1)} %get-tuple-element.99.refs_1_), channel_id=1, source_target_pairs={{0,1},{1,0},{2,3},{3,2},{4,5},{5,4},{6,7},{7,6},{8,9},{9,8},{10,11... | collective-permute-start | bytes 786440 | tf_op jit(solution)/shard_map/ppermute | solution.py:28
  19.0 15.7 %collective-permute-start.10 = (bf16[64,2048]{1,0:T(8,128)(2,1)S(1)}, bf16[64,2048]{1,0:T(8,128)(2,1)}, u32[]{:S(2)}, u32[]{:S(2)}) collective-permute-start(bf16[64,2048]{1,0:T(8,128)(2,1)S(1)} %collective-permute-done.refs_0_), channel_id=1, source_target_pairs={{0,1},{1,0},{2,3},{3,2},{4,5},{5,4},{6,7},{7,6},{8,9},{9,8},{10,11... | collective-permute-start | bytes 786440 | tf_op jit(solution)/shard_map/ppermute | solution.py:28
  19.8 15.0 %collective-permute-start.11 = (bf16[64,2048]{1,0:T(8,128)(2,1)S(1)}, bf16[64,2048]{1,0:T(8,128)(2,1)}, u32[]{:S(2)}, u32[]{:S(2)}) collective-permute-start(bf16[64,2048]{1,0:T(8,128)(2,1)S(1)} %collective-permute-done.3.refs_1_), channel_id=1, source_target_pairs={{0,1},{1,0},{2,3},{3,2},{4,5},{5,4},{6,7},{7,6},{8,9},{9,8},{10,11... | collective-permute-start | bytes 786440 | tf_op jit(solution)/shard_map/ppermute | solution.py:28
  24.7 25.5 %collective-permute-start.2 = (bf16[64,2048]{1,0:T(8,128)(2,1)}, bf16[64,2048]{1,0:T(8,128)(2,1)}, u32[]{:S(2)}, u32[]{:S(2)}) collective-permute-start(bf16[64,2048]{1,0:T(8,128)(2,1)} %collective-permute-done.1.refs_0_), channel_id=1, source_target_pairs={{0,2},{1,3},{2,4},{3,5},{4,6},{5,7},{6,0},{7,1},{8,10},{9,11},{10,... | collective-permute-start | bytes 786440 | tf_op jit(solution)/shard_map/ppermute | solution.py:33
  30.3 20.1 %collective-permute-start.5 = (bf16[64,2048]{1,0:T(8,128)(2,1)}, bf16[64,2048]{1,0:T(8,128)(2,1)}, u32[]{:S(2)}, u32[]{:S(2)}) collective-permute-start(bf16[64,2048]{1,0:T(8,128)(2,1)} %collective-permute-done.4.refs_1_), channel_id=1, source_target_pairs={{0,2},{1,3},{2,4},{3,5},{4,6},{5,7},{6,0},{7,1},{8,10},{9,11},{10,... | collective-permute-start | bytes 786440 | tf_op jit(solution)/shard_map/ppermute | solution.py:33
  34.7 21.7 %collective-permute-start.8 = (bf16[64,2048]{1,0:T(8,128)(2,1)}, bf16[64,2048]{1,0:T(8,128)(2,1)S(1)}, u32[]{:S(2)}, u32[]{:S(2)}) collective-permute-start(bf16[64,2048]{1,0:T(8,128)(2,1)} %collective-permute-done.1.refs_0_), channel_id=1, source_target_pairs={{0,1},{1,0},{2,3},{3,2},{4,5},{5,4},{6,7},{7,6},{8,9},{9,8},{10,11... | collective-permute-start | bytes 786440 | tf_op jit(solution)/shard_map/ppermute | solution.py:28
  34.8 21.6 %collective-permute-start.9 = (bf16[64,2048]{1,0:T(8,128)(2,1)}, bf16[64,2048]{1,0:T(8,128)(2,1)S(1)}, u32[]{:S(2)}, u32[]{:S(2)}) collective-permute-start(bf16[64,2048]{1,0:T(8,128)(2,1)} %collective-permute-done.4.refs_1_), channel_id=1, source_target_pairs={{0,1},{1,0},{2,3},{3,2},{4,5},{5,4},{6,7},{7,6},{8,9},{9,8},{10,11... | collective-permute-start | bytes 786440 | tf_op jit(solution)/shard_map/ppermute | solution.py:28
  72.9 13.8 %collective-permute-start.17 = (bf16[64,2048]{1,0:T(8,128)(2,1)S(1)}, bf16[64,2048]{1,0:T(8,128)(2,1)S(1)}, u32[]{:S(2)}, u32[]{:S(2)}) collective-permute-start(bf16[64,2048]{1,0:T(8,128)(2,1)S(1)} %out_project.13), channel_id=1, source_target_pairs={{0,2},{1,3},{2,4},{3,5},{4,6},{5,7},{6,0},{7,1},{8,10},{9,11},{10,... | collective-permute-start | bytes 786440 | tf_op jit(solution)/shard_map/ppermute | solution.py:33
  89.0 14.4 %collective-permute-start.21 = (bf16[64,2048]{1,0:T(8,128)(2,1)S(1)}, bf16[64,2048]{1,0:T(8,128)(2,1)S(1)}, u32[]{:S(2)}, u32[]{:S(2)}) collective-permute-start(bf16[64,2048]{1,0:T(8,128)(2,1)S(1)} %add_convert_fusion.5), channel_id=1, source_target_pairs={{0,2},{1,3},{2,4},{3,5},{4,6},{5,7},{6,0},{7,1},{8,10},{9,11},{10,... | collective-permute-start | bytes 786440 | tf_op jit(solution)/shard_map/ppermute | solution.py:33
  114.6 12.8 %collective-permute-start.23 = (bf16[64,2048]{1,0:T(8,128)(2,1)S(1)}, bf16[64,2048]{1,0:T(8,128)(2,1)S(1)}, u32[]{:S(2)}, u32[]{:S(2)}) collective-permute-start(bf16[64,2048]{1,0:T(8,128)(2,1)S(1)} %get-tuple-element.73), channel_id=1, source_target_pairs={{0,10},{1,11},{2,12},{3,13},{4,14},{5,15},{6,8},{7,9},{8,18},{9,19... | collective-permute-start | bytes 786440 | tf_op jit(solution)/shard_map/ppermute | solution.py:43
  115.8 15.0 %collective-permute-start.26 = (bf16[64,2048]{1,0:T(8,128)(2,1)S(1)}, bf16[64,2048]{1,0:T(8,128)(2,1)S(1)}, u32[]{:S(2)}, u32[]{:S(2)}) collective-permute-start(bf16[64,2048]{1,0:T(8,128)(2,1)S(1)} %get-tuple-element.74), channel_id=1, source_target_pairs={{0,10},{1,11},{2,12},{3,13},{4,14},{5,15},{6,8},{7,9},{8,18},{9,19... | collective-permute-start | bytes 786440 | tf_op jit(solution)/shard_map/ppermute | solution.py:43
  133.8 12.9 %collective-permute-start.27 = (bf16[64,2048]{1,0:T(8,128)(2,1)S(1)}, bf16[64,2048]{1,0:T(8,128)(2,1)S(1)}, u32[]{:S(2)}, u32[]{:S(2)}) collective-permute-start(bf16[64,2048]{1,0:T(8,128)(2,1)S(1)} %collective-permute-done.26.refs_1_), channel_id=1, source_target_pairs={{0,2},{1,3},{2,4},{3,5},{4,6},{5,7},{6,0},{7,1},{8,10},{9,11},{10,... | collective-permute-start | bytes 786440 | tf_op jit(solution)/shard_map/ppermute | solution.py:33
  133.8 12.9 %collective-permute-start.33 = (bf16[64,2048]{1,0:T(8,128)(2,1)S(1)}, bf16[64,2048]{1,0:T(8,128)(2,1)S(1)}, u32[]{:S(2)}, u32[]{:S(2)}) collective-permute-start(bf16[64,2048]{1,0:T(8,128)(2,1)S(1)} %collective-permute-done.23.refs_0_), channel_id=1, source_target_pairs={{0,1},{1,0},{2,3},{3,2},{4,5},{5,4},{6,7},{7,6},{8,9},{9,8},{10,11... | collective-permute-start | bytes 786440 | tf_op jit(solution)/shard_map/ppermute | solution.py:28
  146.7 12.8 %collective-permute-start.28 = (bf16[64,2048]{1,0:T(8,128)(2,1)S(1)}, bf16[64,2048]{1,0:T(8,128)(2,1)S(1)}, u32[]{:S(2)}, u32[]{:S(2)}) collective-permute-start(bf16[64,2048]{1,0:T(8,128)(2,1)S(1)} %collective-permute-done.27.refs_1_), channel_id=1, source_target_pairs={{0,2},{1,3},{2,4},{3,5},{4,6},{5,7},{6,0},{7,1},{8,10},{9,11},{10,... | collective-permute-start | bytes 786440 | tf_op jit(solution)/shard_map/ppermute | solution.py:33
  146.7 18.3 %collective-permute-start.34 = (bf16[64,2048]{1,0:T(8,128)(2,1)S(1)}, bf16[64,2048]{1,0:T(8,128)(2,1)S(1)}, u32[]{:S(2)}, u32[]{:S(2)}) collective-permute-start(bf16[64,2048]{1,0:T(8,128)(2,1)S(1)} %collective-permute-done.26.refs_1_), channel_id=1, source_target_pairs={{0,1},{1,0},{2,3},{3,2},{4,5},{5,4},{6,7},{7,6},{8,9},{9,8},{10,11... | collective-permute-start | bytes 786440 | tf_op jit(solution)/shard_map/ppermute | solution.py:28
  146.8 20.5 %collective-permute-start.31 = (bf16[64,2048]{1,0:T(8,128)(2,1)S(1)}, bf16[64,2048]{1,0:T(8,128)(2,1)S(1)}, u32[]{:S(2)}, u32[]{:S(2)}) collective-permute-start(bf16[64,2048]{1,0:T(8,128)(2,1)S(1)} %collective-permute-done.24.refs_0_), channel_id=1, source_target_pairs={{0,1},{1,0},{2,3},{3,2},{4,5},{5,4},{6,7},{7,6},{8,9},{9,8},{10,11... | collective-permute-start | bytes 786440 | tf_op jit(solution)/shard_map/ppermute | solution.py:28
  147.3 20.0 %collective-permute-start.32 = (bf16[64,2048]{1,0:T(8,128)(2,1)S(1)}, bf16[64,2048]{1,0:T(8,128)(2,1)S(1)}, u32[]{:S(2)}, u32[]{:S(2)}) collective-permute-start(bf16[64,2048]{1,0:T(8,128)(2,1)S(1)} %collective-permute-done.27.refs_1_), channel_id=1, source_target_pairs={{0,1},{1,0},{2,3},{3,2},{4,5},{5,4},{6,7},{7,6},{8,9},{9,8},{10,11... | collective-permute-start | bytes 786440 | tf_op jit(solution)/shard_map/ppermute | solution.py:28
  154.9 14.5 %collective-permute-start.29 = (bf16[64,2048]{1,0:T(8,128)(2,1)S(1)}, bf16[64,2048]{1,0:T(8,128)(2,1)S(1)}, u32[]{:S(2)}, u32[]{:S(2)}) collective-permute-start(bf16[64,2048]{1,0:T(8,128)(2,1)S(1)} %collective-permute-done.25.refs_0_), channel_id=1, source_target_pairs={{0,1},{1,0},{2,3},{3,2},{4,5},{5,4},{6,7},{7,6},{8,9},{9,8},{10,11... | collective-permute-start | bytes 786440 | tf_op jit(solution)/shard_map/ppermute | solution.py:28
  182.6 14.9 %collective-permute-start.41 = (bf16[64,2048]{1,0:T(8,128)(2,1)S(1)}, bf16[64,2048]{1,0:T(8,128)(2,1)S(1)}, u32[]{:S(2)}, u32[]{:S(2)}) collective-permute-start(bf16[64,2048]{1,0:T(8,128)(2,1)S(1)} %out_project.18), channel_id=1, source_target_pairs={{0,2},{1,3},{2,4},{3,5},{4,6},{5,7},{6,0},{7,1},{8,10},{9,11},{10,... | collective-permute-start | bytes 786440 | tf_op jit(solution)/shard_map/ppermute | solution.py:33
  185.8 12.9 %collective-permute-start.44 = (bf16[64,2048]{1,0:T(8,128)(2,1)S(1)}, bf16[64,2048]{1,0:T(8,128)(2,1)S(1)}, u32[]{:S(2)}, u32[]{:S(2)}) collective-permute-start(bf16[64,2048]{1,0:T(8,128)(2,1)S(1)} %out_project.19), channel_id=1, source_target_pairs={{0,2},{1,3},{2,4},{3,5},{4,6},{5,7},{6,0},{7,1},{8,10},{9,11},{10,... | collective-permute-start | bytes 786440 | tf_op jit(solution)/shard_map/ppermute | solution.py:33
  198.7 15.5 %collective-permute-start.45 = (bf16[64,2048]{1,0:T(8,128)(2,1)S(1)}, bf16[64,2048]{1,0:T(8,128)(2,1)S(1)}, u32[]{:S(2)}, u32[]{:S(2)}) collective-permute-start(bf16[64,2048]{1,0:T(8,128)(2,1)S(1)} %add_convert_fusion.1), channel_id=1, source_target_pairs={{0,2},{1,3},{2,4},{3,5},{4,6},{5,7},{6,0},{7,1},{8,10},{9,11},{10,... | collective-permute-start | bytes 786440 | tf_op jit(solution)/shard_map/ppermute | solution.py:33
  (38 other events, 250.8 us)
where the time goes:
time: 227 us; the launch traced here: 226 us
  waiting for transfers between devices  104 us (46%)
  Pallas kernels  67.6 us (30%)
  starting transfers between devices  25.8 us (11%)
  local copies, waits for them, and re-layouts  21.1 us (9%)
  matrix products  4.36 us (2%)
  other arithmetic  3.45 us (2%)
    ppermute x22, waiting for transfers between devices, chip_ring(): lax.ppermute(value, 'seq', [(i, (i + 2) % count) for i in range(count)])  77.6 us
    pallas_call x10, Pallas kernels, out_project(): pl.pallas_call(functools.partial(out_kernel, steps=steps, chips=chips, fi...  34.9 us
    ppermute x4, waiting for transfers between devices, next_section(): return lax.ppermute(value, ('section', 'seq'), pairs)  23.4 us
    unnamed x31, local copies, waits for them, and re-layouts  20 us
    pallas_call x8, Pallas kernels, project(): pl.pallas_call(functools.partial(project_kernel, steps=steps, chips=chips...  18.6 us
    ppermute x22, starting transfers between devices, chip_ring(): lax.ppermute(value, 'seq', [(i, (i + 2) % count) for i in range(count)])  15.9 us
    pallas_call x2, Pallas kernels, mix(): pl.pallas_call(mix_kernel, grid=(length // BLOCK,), in_specs=[IN_SMEM] +...  12.2 us
    ppermute x4, starting transfers between devices, next_section(): return lax.ppermute(value, ('section', 'seq'), pairs)  5.4 us
  transfers between devices with their start and end apart: 47, of which 23 were waited for; matrix products, arithmetic and copies ran while one was open for 7% of the time, Pallas kernels for 24%

commit v1 on v0

--- a/solution.py
+++ b/solution.py
@@ -58,7 +58,7 @@
 
 def project_kernel(where, *refs, steps, chips):
     xs, refs = refs[: 2 * PIECES], refs[2 * PIECES :]
-    weights, outs = refs[:2], refs[-2:]
+    xz_parts, p_weight, outs = refs[:PIECES], refs[PIECES], refs[-2:]
     core = where[1]
     tokens, depth = xs[0].shape
     start = chip_at(where, steps, chips) * (2 * tokens)
@@ -67,12 +67,11 @@
     tall = [
         jnp.concatenate([xs[i][...], xs[PIECES + i][...]], axis=0) for i in range(PIECES)
     ]
-    for weight, out in zip(weights, outs):
+    p_parts = [p_weight.at[i * depth : (i + 1) * depth, :] for i in range(PIECES)]
+    for weights, out in zip((xz_parts, p_parts), outs):
         total = None
-        for i, x in enumerate(tall):
-            part = jnp.dot(
-                x, weight[i * depth : (i + 1) * depth, :], preferred_element_type=f32
-            )
+        for x, weight in zip(tall, weights):
+            part = jnp.dot(x, weight[...], preferred_element_type=f32)
             total = part if total is None else total + part
         total = total.astype(bf16)
         out[mine, :] = total[:tokens]
@@ -87,13 +86,14 @@
         aliases = {len(args): 0, len(args) + 1: 1}
         args += list(buffers)
         in_specs += [IN_VMEM] * 2
-    width = weights[0].shape[0]
-    columns = sum(weight.shape[1] for weight in weights)
+    width = weights[-1].shape[0]
+    n_out = [weights[0].shape[1], weights[-1].shape[1]]
+    columns = sum(n_out)
     return pl.pallas_call(
         functools.partial(project_kernel, steps=steps, chips=chips),
         in_specs=in_specs,
         out_specs=[IN_VMEM] * 2,
-        out_shape=[jax.ShapeDtypeStruct((length, weight.shape[1]), bf16) for weight in weights],
+        out_shape=[jax.ShapeDtypeStruct((length, n), bf16) for n in n_out],
         input_output_aliases=aliases,
         compiler_params=PARAMS,
         cost_estimate=pl.CostEstimate(
@@ -105,22 +105,49 @@
     )(*args)
 
 
-def ready_kernel(where, xz_ref, p_ref, out):
-    del xz_ref, p_ref
+def ready_kernel(where, weight, out):
+    del weight
     out[0] = where[0]
     out[1] = where[1]
 
 
-def ready(where, xz_local, p_local):
-    anywhere = pl.BlockSpec(memory_space=pl.ANY)
+def ready(where, weight):
     return pl.pallas_call(
         ready_kernel,
-        in_specs=[IN_SMEM, anywhere, anywhere],
+        in_specs=[IN_SMEM, pl.BlockSpec(memory_space=pl.ANY)],
         out_specs=IN_SMEM,
         out_shape=jax.ShapeDtypeStruct(where.shape, where.dtype),
         compiler_params=PARAMS,
         name="ready",
-    )(where, xz_local, p_local)
+    )(where, weight)
+
+
+def stage_kernel(upper, lower, out, semaphores):
+    rows = upper.shape[0]
+    copies = [
+        pltpu.make_async_copy(part, out.at[i * rows : (i + 1) * rows, :], semaphores.at[i])
+        for i, part in enumerate((upper, lower))
+    ]
+    for copy in copies:
+        copy.start()
+    for copy in copies:
+        copy.wait()
+
+
+def stage(upper, lower):
+    rows, cols = upper.shape
+    return pl.pallas_call(
+        stage_kernel,
+        in_specs=[pl.BlockSpec(memory_space=pl.ANY)] * 2,
+        out_specs=IN_VMEM,
+        out_shape=jax.ShapeDtypeStruct((2 * rows, cols), upper.dtype),
+        scratch_shapes=[pltpu.SemaphoreType.DMA((2,))],
+        compiler_params=PARAMS,
+        cost_estimate=pl.CostEstimate(
+            flops=0, bytes_accessed=8 * rows * cols, transcendentals=0
+        ),
+        name="stage",
+    )(upper, lower)
 
 
 def spread_of(chans):
@@ -321,7 +348,7 @@
     )(where, xz, p, *tables)
 
 
-def out_kernel(where, g_mine, g_other, w_mine, w_other, *refs, steps, chips, first, count, scale):
+def out_kernel(where, g_mine, g_other, weight, *refs, steps, chips, first, count, scale):
     squares, outs = refs[:-count], refs[-count:]
     rows, tile = outs[0].shape
     at = pl.ds(pl.multiple_of(chip_at(where, steps, chips) * rows, rows), rows)
@@ -329,18 +356,18 @@
     for more in squares[1:]:
         total = total + more[at, 0:1]
     rate = lax.rsqrt(total * scale + 1e-05)
+    both = jnp.concatenate([g_mine[at, :], g_other[at, :]], axis=1)
     for i, out in enumerate(outs):
         cols = slice((first + i) * tile, (first + i + 1) * tile)
-        part = jnp.dot(g_mine[at, :], w_mine[:, cols], preferred_element_type=f32)
-        part = part + jnp.dot(g_other[at, :], w_other[:, cols], preferred_element_type=f32)
+        part = jnp.dot(both, weight[:, cols], preferred_element_type=f32)
         out[...] = (part * rate).astype(out.dtype)
 
 
-def out_project(where, steps, chips, gated, weights, squares, pieces, dtype):
-    chans, cols = weights[0].shape
+def out_project(where, steps, chips, gated, weight, squares, pieces, dtype):
+    chans, cols = weight.shape
     rows = gated[0].shape[0] // chips
     first, count = pieces
-    args = [where, *gated, *weights, *squares]
+    args = [where, *gated, weight, *squares]
     return pl.pallas_call(
         functools.partial(
             out_kernel,
@@ -355,8 +382,8 @@
         out_shape=[jax.ShapeDtypeStruct((rows, cols // PIECES), dtype)] * count,
         compiler_params=PARAMS,
         cost_estimate=pl.CostEstimate(
-            flops=4 * rows * chans * cols * count // PIECES,
-            bytes_accessed=4 * chans * cols * count // PIECES,
+            flops=2 * rows * chans * cols * count // PIECES,
+            bytes_accessed=2 * chans * cols * count // PIECES,
             transcendentals=0,
         ),
         name="out_project",
@@ -399,7 +426,11 @@
     entering = in_pieces(inflow[0])
     arriving = [chip_ring(x) for x in entering]
 
-    xz_local = xz_weight[0].reshape(width, 2 * chan_dev)
+    def regrouped(weight, i):
+        rows = slice(i * piece, (i + 1) * piece)
+        return weight[0, rows].reshape(piece, 2 * chan_dev)
+
+    xz_parts = [regrouped(xz_weight, 0)]
     column = lax.broadcasted_iota(jnp.int32, (proj_weight.shape[2], 2 * LANES), 1)
     source = jnp.where(
         column < STATE,
@@ -413,25 +444,32 @@
     chosen = (lax.broadcasted_iota(jnp.int32, column.shape, 0) == source) & (
         column < 2 * STATE + heads_dev
     )
+    where_ready = ready(where, xz_parts[0])
     p_local = jnp.dot(
-        proj_weight[0], chosen.astype(bf16), preferred_element_type=f32
+        after(proj_weight[0], where_ready), chosen.astype(bf16), preferred_element_type=f32
     ).astype(bf16)
-    where_ready = ready(where, xz_local, p_local)
+    xz_parts += [regrouped(after(xz_weight, where_ready), i) for i in range(1, PIECES)]
     tables = tables_of(
-        where, (conv_weight[0], conv_bias, step_bias, decay_log, skip_weight, norm_gain), chan_dev
-    )
-    out_weights = (out_weight[0], swapped(out_weight[0], 1))
-
-    def layer(held, arriving):
+        where_ready, (conv_weight[0], conv_bias, step_bias, decay_log, skip_weight, norm_gain), chan_dev
+    )
+    out_swapped = swapped(out_weight[0], 1)
+
+    def layer(held, arriving, staged=None):
         buffers = None
+        indices = where_ready
+        pausing = staged is not None
         for step in range(chips):
+            if step == chips - 1 and staged is None:
+                staged = stage(after(out_weight[0], buffers), out_swapped)
             if step == 1:
                 held = arriving
             elif step > 1:
+                if pausing:
+                    indices = ready(indices, held[0])
                 held = [chip_ring(x) for x in held]
             other = [swapped(part, 1) for part in held]
             buffers = project(
-                where_ready, step, chips, held + other, (xz_local, p_local), length, buffers
+                indices, step, chips, held + other, (*xz_parts, p_local), length, buffers
             )
         near, far, near_squares, far_squares = mix(where, *buffers, tables)
         gated = (near, swapped(far, 1))
@@ -439,29 +477,36 @@
         for mask in range(0, group_members, 2):
             squares.append(swapped(near_squares, mask) if mask else near_squares)
             squares.append(swapped(far_squares, mask ^ 1))
-        running = None
+        running = parts = None
         for step in range(1, chips + 1):
+            gate = where if parts is None else after(where, parts)
             calls = [(i, 1) for i in range(PIECES)] if step == 1 else [(0, PIECES)]
             parts = []
             for call in calls:
                 parts += out_project(
-                    where, step, chips, gated, out_weights, squares, call,
+                    after(gate, parts) if parts else gate, step, chips, gated, staged, squares, call,
                     bf16 if step == 1 else f32,
                 )
             if running is not None:
-                parts = [part + came.astype(f32) for part, came in zip(parts, running)]
+                sums = []
+                for part, came in zip(parts, running):
+                    came = after(came, sums) if sums else came
+                    sums.append(part + came.astype(f32))
+                parts = sums
             if step < chips:
-                running = [chip_ring(part.astype(bf16)) for part in parts]
-        return parts
-
-    first = layer(entering, arriving)
-    leaving = [
-        jnp.where(position == sections - 1, new, part.astype(bf16))
-        for new, part in zip(in_pieces(fresh[0]), first)
-    ]
+                parts = [part.astype(bf16) for part in parts]
+                running = [chip_ring(x) for x in parts]
+        return parts, staged
+
+    first, staged = layer(entering, arriving)
+    leaving = []
+    for i, new in enumerate(in_pieces(fresh[0])):
+        if leaving:
+            first[i] = after(first[i], leaving)
+        leaving.append(jnp.where(position == sections - 1, new, first[i].astype(bf16)))
     ahead = [next_section(x, 1) for x in leaving]
     level = [next_section(x, 0) for x in after(leaving, ahead)]
-    second = layer(level, ahead)
+    second, _ = layer(level, ahead, staged)
     return jnp.stack([jnp.concatenate(first, axis=1), jnp.concatenate(second, axis=1)])[None]
 
 

time: 227 us -> 204 us (0.90)
  Pallas kernels: 67.6 us -> 55.1 us
  starting transfers between devices: 25.8 us -> 15 us
  waiting for transfers between devices: 104 us -> 114 us
  local copies, waits for them, and re-layouts: 21.1 us -> 14.6 us
  matrix products: 4.36 us -> 1.94 us
    ppermute x22, waiting for transfers between devices: 77.6 us -> 94.6 us  [chip_ring(): lax.ppermute(value, 'seq', [(i, (i + 2) % count) for i in range(count)])]
    pallas_call x10, Pallas kernels: 34.9 us -> 18.3 us  [out_project(): pl.pallas_call(functools.partial(out_kernel, steps=steps, chips=chips, fi...]
    unnamed x31 -> x50, local copies, waits for them, and re-layouts: 20 us -> 9.73 us
    ppermute x22, starting transfers between devices: 15.9 us -> 6.88 us  [chip_ring(): lax.ppermute(value, 'seq', [(i, (i + 2) % count) for i in range(count)])]
    ppermute x4, waiting for transfers between devices: 23.4 us -> 17.6 us  [next_section(): return lax.ppermute(value, ('section', 'seq'), pairs)]
    pallas_call x1 -> x4, Pallas kernels: 1.14 us -> 5.89 us  [the longest x3 3.41 us: ready(): pl.pallas_call(ready_kernel, in_specs=[IN_SMEM, pl.BlockSpec(memory_space...]
    slice x0 -> x4, local copies, waits for them, and re-layouts: none -> 3.82 us  [regrouped(): return weight[0, rows].reshape(piece, 2 * chan_dev)]
    dot_general x1, matrix products: 4.36 us -> 1.94 us  [on_device(): jnp.dot(after(proj_weight[0], where_ready), chosen.astype(bf16), preferre...]
  transfers between devices with their start and end apart: 47 -> 47, of which waited for: 23 -> 25; matrix products, arithmetic and copies ran while one was open for 7% -> 3% of each run, Pallas kernels for 24% -> 22%
where the time goes in v1:
time: 204 us; the launch traced here: 203 us
  waiting for transfers between devices  114 us (56%)
  Pallas kernels  55.1 us (27%)
  starting transfers between devices  15 us (7%)
  local copies, waits for them, and re-layouts  14.6 us (7%)
  other arithmetic  2.46 us (1%)
    ppermute x22, waiting for transfers between devices, chip_ring(): lax.ppermute(value, 'seq', [(i, (i + 2) % count) for i in range(count)])  94.6 us
    pallas_call x10, Pallas kernels, out_project(): pl.pallas_call(functools.partial(out_kernel, steps=steps, chips=chips, fi...  18.3 us
    pallas_call x8, Pallas kernels, project(): pl.pallas_call(functools.partial(project_kernel, steps=steps, chips=chips...  18 us
    ppermute x4, waiting for transfers between devices, next_section(): return lax.ppermute(value, ('section', 'seq'), pairs)  17.6 us
    pallas_call x2, Pallas kernels, mix(): pl.pallas_call(mix_kernel, grid=(length // BLOCK,), in_specs=[IN_SMEM] +...  12.1 us
    unnamed x50, local copies, waits for them, and re-layouts  9.73 us
    ppermute x22, starting transfers between devices, chip_ring(): lax.ppermute(value, 'seq', [(i, (i + 2) % count) for i in range(count)])  6.88 us
    ppermute x4, starting transfers between devices, next_section(): return lax.ppermute(value, ('section', 'seq'), pairs)  4.99 us
  transfers between devices with their start and end apart: 47, of which 25 were waited for; matrix products, arithmetic and copies ran while one was open for 3% of the time, Pallas kernels for 22%

profile of v1, /device:TPU:0, one launch (start us, length us, event | category | flops | bytes accessed | tf_op | source)
XLA Modules:
  0.0 203.3 jit_solution(4077255880712612618)
XLA Ops:
  6.0 7.4 %collective-permute-done.3.refs_1_ = bf16[64,2048]{1,0:T(8,128)(2,1)S(1)} collective-permute-done((bf16[64,2048]{1,0:T(8,128)(2,1)S(1)}, bf16[64,2048]{1,0:T(8,128)(2,1)S(1)}, u32[]{:S(2)}, u32[]{:S(2)}) %collective-permute-start.3) | collective-permute-done | bytes 262176 | tf_op jit(solution)/shard_map/ppermute | solution.py:33
  13.4 5.6 %collective-permute-done.refs_0_ = bf16[64,2048]{1,0:T(8,128)(2,1)S(1)} collective-permute-done((bf16[64,2048]{1,0:T(8,128)(2,1)S(1)}, bf16[64,2048]{1,0:T(8,128)(2,1)S(1)}, u32[]{:S(2)}, u32[]{:S(2)}) %collective-permute-start) | collective-permute-done | bytes 262176 | tf_op jit(solution)/shard_map/ppermute | solution.py:33
  26.3 3.9 %collective-permute-done.1.refs_0_ = bf16[64,2048]{1,0:T(8,128)(2,1)} collective-permute-done((bf16[64,2048]{1,0:T(8,128)(2,1)S(1)}, bf16[64,2048]{1,0:T(8,128)(2,1)}, u32[]{:S(2)}, u32[]{:S(2)}) %collective-permute-start.1) | collective-permute-done | bytes 262176 | tf_op jit(solution)/shard_map/ppermute | solution.py:33
  37.7 4.1 %collective-permute-done.2.refs_0_ = bf16[64,2048]{1,0:T(8,128)(2,1)S(1)} collective-permute-done((bf16[64,2048]{1,0:T(8,128)(2,1)}, bf16[64,2048]{1,0:T(8,128)(2,1)S(1)}, u32[]{:S(2)}, u32[]{:S(2)}) %collective-permute-start.2) | collective-permute-done | bytes 262176 | tf_op jit(solution)/shard_map/ppermute | solution.py:33
  51.2 6.0 %mix.2 = (bf16[256,512]{1,0:T(8,128)(2,1)S(1)}, bf16[256,512]{1,0:T(8,128)(2,1)S(1)}, f32[256,128]{1,0:T(8,128)S(1)}, f32[256,128]{1,0:T(8,128)S(1)}) custom-call(s32[2]{0:T(128)S(1)} %pad_add_fusion.where, bf16[512,1024]{1,0:T(8,128)(2,1)S(1)} %get-tuple-element.75.xz_ref, bf16[512,256]{1,0:T(8,128)(2,1)S(1)} %get-tuple-element.76.p_ref, ...), custom_call_target="tpu_custom_call" | custom-call | flops 536870912 | bytes 1835008 | tf_op jit(solution)/shard_map/mix/pallas_call | solution.py:328
  63.7 3.4 %copy-done.1 = bf16[1024,4096]{1,0:T(8,128)(2,1)S(1)} copy-done((bf16[1024,4096]{1,0:T(8,128)(2,1)S(1)}, bf16[1024,4096]{1,0:T(8,128)(2,1)}, u32[]{:S(2)}) %copy-start.1) | copy-done | bytes 8388632
  71.7 2.9 %collective-permute-done.17 = bf16[64,2048]{1,0:T(8,128)(2,1)S(1)} collective-permute-done((bf16[64,2048]{1,0:T(8,128)(2,1)S(1)}, bf16[64,2048]{1,0:T(8,128)(2,1)S(1)}, u32[]{:S(2)}, u32[]{:S(2)}) %collective-permute-start.17) | collective-permute-done | bytes 262176 | tf_op jit(solution)/shard_map/ppermute | solution.py:33
  74.8 5.5 %collective-permute-done.18 = bf16[64,2048]{1,0:T(8,128)(2,1)S(1)} collective-permute-done((bf16[64,2048]{1,0:T(8,128)(2,1)S(1)}, bf16[64,2048]{1,0:T(8,128)(2,1)S(1)}, u32[]{:S(2)}, u32[]{:S(2)}) %collective-permute-start.18) | collective-permute-done | bytes 262176 | tf_op jit(solution)/shard_map/ppermute | solution.py:33
  82.6 3.3 %collective-permute-done.19 = bf16[64,2048]{1,0:T(8,128)(2,1)S(1)} collective-permute-done((bf16[64,2048]{1,0:T(8,128)(2,1)S(1)}, bf16[64,2048]{1,0:T(8,128)(2,1)S(1)}, u32[]{:S(2)}, u32[]{:S(2)}) %collective-permute-start.19) | collective-permute-done | bytes 262176 | tf_op jit(solution)/shard_map/ppermute | solution.py:33
  86.0 5.5 %collective-permute-done.20 = bf16[64,2048]{1,0:T(8,128)(2,1)S(1)} collective-permute-done((bf16[64,2048]{1,0:T(8,128)(2,1)S(1)}, bf16[64,2048]{1,0:T(8,128)(2,1)S(1)}, u32[]{:S(2)}, u32[]{:S(2)}) %collective-permute-start.20) | collective-permute-done | bytes 262176 | tf_op jit(solution)/shard_map/ppermute | solution.py:33
  93.8 3.3 %collective-permute-done.21 = bf16[64,2048]{1,0:T(8,128)(2,1)S(1)} collective-permute-done((bf16[64,2048]{1,0:T(8,128)(2,1)S(1)}, bf16[64,2048]{1,0:T(8,128)(2,1)S(1)}, u32[]{:S(2)}, u32[]{:S(2)}) %collective-permute-start.21) | collective-permute-done | bytes 262176 | tf_op jit(solution)/shard_map/ppermute | solution.py:33
  97.3 5.0 %collective-permute-done.22 = bf16[64,2048]{1,0:T(8,128)(2,1)S(1)} collective-permute-done((bf16[64,2048]{1,0:T(8,128)(2,1)S(1)}, bf16[64,2048]{1,0:T(8,128)(2,1)S(1)}, u32[]{:S(2)}, u32[]{:S(2)}) %collective-permute-start.22) | collective-permute-done | bytes 262176 | tf_op jit(solution)/shard_map/ppermute | solution.py:33
  104.2 10.9 %collective-permute-done.26.refs_1_ = bf16[64,2048]{1,0:T(8,128)(2,1)S(1)} collective-permute-done((bf16[64,2048]{1,0:T(8,128)(2,1)S(1)}, bf16[64,2048]{1,0:T(8,128)(2,1)S(1)}, u32[]{:S(2)}, u32[]{:S(2)}) %collective-permute-start.26) | collective-permute-done | bytes 262176 | tf_op jit(solution)/shard_map/ppermute | solution.py:43
  115.2 4.2 %collective-permute-done.23.weight.refs_0_ = bf16[64,2048]{1,0:T(8,128)(2,1)S(1)} collective-permute-done((bf16[64,2048]{1,0:T(8,128)(2,1)S(1)}, bf16[64,2048]{1,0:T(8,128)(2,1)S(1)}, u32[]{:S(2)}, u32[]{:S(2)}) %collective-permute-start.23) | collective-permute-done | bytes 262176 | tf_op jit(solution)/shard_map/ppermute | solution.py:43
  122.5 7.8 %collective-permute-done.27.refs_1_ = bf16[64,2048]{1,0:T(8,128)(2,1)S(1)} collective-permute-done((bf16[64,2048]{1,0:T(8,128)(2,1)S(1)}, bf16[64,2048]{1,0:T(8,128)(2,1)S(1)}, u32[]{:S(2)}, u32[]{:S(2)}) %collective-permute-start.27) | collective-permute-done | bytes 262176 | tf_op jit(solution)/shard_map/ppermute | solution.py:33
  132.8 3.1 %collective-permute-done.24.weight.refs_0_ = bf16[64,2048]{1,0:T(8,128)(2,1)S(1)} collective-permute-done((bf16[64,2048]{1,0:T(8,128)(2,1)S(1)}, bf16[64,2048]{1,0:T(8,128)(2,1)S(1)}, u32[]{:S(2)}, u32[]{:S(2)}) %collective-permute-start.24) | collective-permute-done | bytes 262176 | tf_op jit(solution)/shard_map/ppermute | solution.py:33
  136.0 5.0 %collective-permute-done.28.refs_1_ = bf16[64,2048]{1,0:T(8,128)(2,1)S(1)} collective-permute-done((bf16[64,2048]{1,0:T(8,128)(2,1)S(1)}, bf16[64,2048]{1,0:T(8,128)(2,1)S(1)}, u32[]{:S(2)}, u32[]{:S(2)}) %collective-permute-start.28) | collective-permute-done | bytes 262176 | tf_op jit(solution)/shard_map/ppermute | solution.py:33
  153.8 6.0 %mix.3 = (bf16[256,512]{1,0:T(8,128)(2,1)S(1)}, bf16[256,512]{1,0:T(8,128)(2,1)S(1)}, f32[256,128]{1,0:T(8,128)S(1)}, f32[256,128]{1,0:T(8,128)S(1)}) custom-call(s32[2]{0:T(128)S(1)} %pad_add_fusion.where, bf16[512,1024]{1,0:T(8,128)(2,1)S(1)} %get-tuple-element.110.xz_ref, bf16[512,256]{1,0:T(8,128)(2,1)S(1)} %get-tuple-element.111.p_ref, ...), custom_call_target="tpu_custom_call" | custom-call | flops 536870912 | bytes 1835008 | tf_op jit(solution)/shard_map/mix/pallas_call | solution.py:328
  166.9 7.3 %collective-permute-done.41 = bf16[64,2048]{1,0:T(8,128)(2,1)S(1)} collective-permute-done((bf16[64,2048]{1,0:T(8,128)(2,1)S(1)}, bf16[64,2048]{1,0:T(8,128)(2,1)S(1)}, u32[]{:S(2)}, u32[]{:S(2)}) %collective-permute-start.41) | collective-permute-done | bytes 262176 | tf_op jit(solution)/shard_map/ppermute | solution.py:33
  174.4 5.5 %collective-permute-done.42 = bf16[64,2048]{1,0:T(8,128)(2,1)S(1)} collective-permute-done((bf16[64,2048]{1,0:T(8,128)(2,1)S(1)}, bf16[64,2048]{1,0:T(8,128)(2,1)S(1)}, u32[]{:S(2)}, u32[]{:S(2)}) %collective-permute-start.42) | collective-permute-done | bytes 262176 | tf_op jit(solution)/shard_map/ppermute | solution.py:33
  182.1 3.4 %collective-permute-done.43 = bf16[64,2048]{1,0:T(8,128)(2,1)S(1)} collective-permute-done((bf16[64,2048]{1,0:T(8,128)(2,1)S(1)}, bf16[64,2048]{1,0:T(8,128)(2,1)S(1)}, u32[]{:S(2)}, u32[]{:S(2)}) %collective-permute-start.43) | collective-permute-done | bytes 262176 | tf_op jit(solution)/shard_map/ppermute | solution.py:33
  185.6 5.5 %collective-permute-done.44 = bf16[64,2048]{1,0:T(8,128)(2,1)S(1)} collective-permute-done((bf16[64,2048]{1,0:T(8,128)(2,1)S(1)}, bf16[64,2048]{1,0:T(8,128)(2,1)S(1)}, u32[]{:S(2)}, u32[]{:S(2)}) %collective-permute-start.44) | collective-permute-done | bytes 262176 | tf_op jit(solution)/shard_map/ppermute | solution.py:33
  193.3 3.4 %collective-permute-done.45 = bf16[64,2048]{1,0:T(8,128)(2,1)S(1)} collective-permute-done((bf16[64,2048]{1,0:T(8,128)(2,1)S(1)}, bf16[64,2048]{1,0:T(8,128)(2,1)S(1)}, u32[]{:S(2)}, u32[]{:S(2)}) %collective-permute-start.45) | collective-permute-done | bytes 262176 | tf_op jit(solution)/shard_map/ppermute | solution.py:33
  196.8 5.0 %collective-permute-done.46 = bf16[64,2048]{1,0:T(8,128)(2,1)S(1)} collective-permute-done((bf16[64,2048]{1,0:T(8,128)(2,1)S(1)}, bf16[64,2048]{1,0:T(8,128)(2,1)S(1)}, u32[]{:S(2)}, u32[]{:S(2)}) %collective-permute-start.46) | collective-permute-done | bytes 262176 | tf_op jit(solution)/shard_map/ppermute | solution.py:33
  (174 shorter events, 79.5 us)
Async XLA Ops:
  0.0 57.8 %collective-permute-start.15 = (bf16[512,4096]{1,0:T(8,128)(2,1)}, bf16[512,4096]{1,0:T(8,128)(2,1)}, u32[]{:S(2)}, u32[]{:S(2)}) collective-permute-start(bf16[512,4096]{1,0:T(8,128)(2,1)} %bitcast.39), channel_id=1, source_target_pairs={{0,1},{1,0},{2,3},{3,2},{4,5},{5,4},{6,7},{7,6},{8,9},{9,8},{10,11... | collective-permute-start | bytes 12582920 | tf_op jit(solution)/shard_map/ppermute | solution.py:28
  1.6 11.8 %collective-permute-start.3 = (bf16[64,2048]{1,0:T(8,128)(2,1)S(1)}, bf16[64,2048]{1,0:T(8,128)(2,1)S(1)}, u32[]{:S(2)}, u32[]{:S(2)}) collective-permute-start(bf16[64,2048]{1,0:T(8,128)(2,1)S(1)} %get-tuple-element.131.refs_1_), channel_id=1, source_target_pairs={{0,2},{1,3},{2,4},{3,5},{4,6},{5,7},{6,0},{7,1},{8,10},{9,11},{10,... | collective-permute-start | bytes 786440 | tf_op jit(solution)/shard_map/ppermute | solution.py:33
  4.4 14.6 %collective-permute-start = (bf16[64,2048]{1,0:T(8,128)(2,1)S(1)}, bf16[64,2048]{1,0:T(8,128)(2,1)S(1)}, u32[]{:S(2)}, u32[]{:S(2)}) collective-permute-start(bf16[64,2048]{1,0:T(8,128)(2,1)S(1)} %get-tuple-element.132.refs_0_), channel_id=1, source_target_pairs={{0,2},{1,3},{2,4},{3,5},{4,6},{5,7},{6,0},{7,1},{8,10},{9,11},{10,... | collective-permute-start | bytes 786440 | tf_op jit(solution)/shard_map/ppermute | solution.py:33
  6.0 13.0 %collective-permute-start.12 = (bf16[64,2048]{1,0:T(8,128)(2,1)S(1)}, bf16[64,2048]{1,0:T(8,128)(2,1)S(1)}, u32[]{:S(2)}, u32[]{:S(2)}) collective-permute-start(bf16[64,2048]{1,0:T(8,128)(2,1)S(1)} %get-tuple-element.132.refs_0_), channel_id=1, source_target_pairs={{0,1},{1,0},{2,3},{3,2},{4,5},{5,4},{6,7},{7,6},{8,9},{9,8},{10,11... | collective-permute-start | bytes 786440 | tf_op jit(solution)/shard_map/ppermute | solution.py:28
  13.4 11.3 %collective-permute-start.11 = (bf16[64,2048]{1,0:T(8,128)(2,1)S(1)}, bf16[64,2048]{1,0:T(8,128)(2,1)S(1)}, u32[]{:S(2)}, u32[]{:S(2)}) collective-permute-start(bf16[64,2048]{1,0:T(8,128)(2,1)S(1)} %collective-permute-done.3.refs_1_), channel_id=1, source_target_pairs={{0,1},{1,0},{2,3},{3,2},{4,5},{5,4},{6,7},{7,6},{8,9},{9,8},{10,11... | collective-permute-start | bytes 786440 | tf_op jit(solution)/shard_map/ppermute | solution.py:28
  13.4 11.3 %collective-permute-start.4 = (bf16[64,2048]{1,0:T(8,128)(2,1)S(1)}, bf16[64,2048]{1,0:T(8,128)(2,1)}, u32[]{:S(2)}, u32[]{:S(2)}) collective-permute-start(bf16[64,2048]{1,0:T(8,128)(2,1)S(1)} %collective-permute-done.3.refs_1_), channel_id=1, source_target_pairs={{0,2},{1,3},{2,4},{3,5},{4,6},{5,7},{6,0},{7,1},{8,10},{9,11},{10,... | collective-permute-start | bytes 786440 | tf_op jit(solution)/shard_map/ppermute | solution.py:33
  24.7 21.5 %collective-permute-start.9 = (bf16[64,2048]{1,0:T(8,128)(2,1)}, bf16[64,2048]{1,0:T(8,128)(2,1)S(1)}, u32[]{:S(2)}, u32[]{:S(2)}) collective-permute-start(bf16[64,2048]{1,0:T(8,128)(2,1)} %collective-permute-done.4.refs_1_), channel_id=1, source_target_pairs={{0,1},{1,0},{2,3},{3,2},{4,5},{5,4},{6,7},{7,6},{8,9},{9,8},{10,11... | collective-permute-start | bytes 786440 | tf_op jit(solution)/shard_map/ppermute | solution.py:28
  25.4 11.8 %collective-permute-start.5 = (bf16[64,2048]{1,0:T(8,128)(2,1)}, bf16[64,2048]{1,0:T(8,128)(2,1)S(1)}, u32[]{:S(2)}, u32[]{:S(2)}) collective-permute-start(bf16[64,2048]{1,0:T(8,128)(2,1)} %collective-permute-done.4.refs_1_), channel_id=1, source_target_pairs={{0,2},{1,3},{2,4},{3,5},{4,6},{5,7},{6,0},{7,1},{8,10},{9,11},{10,... | collective-permute-start | bytes 786440 | tf_op jit(solution)/shard_map/ppermute | solution.py:33
  30.1 16.1 %collective-permute-start.8 = (bf16[64,2048]{1,0:T(8,128)(2,1)}, bf16[64,2048]{1,0:T(8,128)(2,1)S(1)}, u32[]{:S(2)}, u32[]{:S(2)}) collective-permute-start(bf16[64,2048]{1,0:T(8,128)(2,1)} %collective-permute-done.1.refs_0_), channel_id=1, source_target_pairs={{0,1},{1,0},{2,3},{3,2},{4,5},{5,4},{6,7},{7,6},{8,9},{9,8},{10,11... | collective-permute-start | bytes 786440 | tf_op jit(solution)/shard_map/ppermute | solution.py:28
  37.2 11.7 %collective-permute-start.7 = (bf16[64,2048]{1,0:T(8,128)(2,1)S(1)}, bf16[64,2048]{1,0:T(8,128)(2,1)S(1)}, u32[]{:S(2)}, u32[]{:S(2)}) collective-permute-start(bf16[64,2048]{1,0:T(8,128)(2,1)S(1)} %collective-permute-done.5.refs_1_), channel_id=1, source_target_pairs={{0,1},{1,0},{2,3},{3,2},{4,5},{5,4},{6,7},{7,6},{8,9},{9,8},{10,11... | collective-permute-start | bytes 786440 | tf_op jit(solution)/shard_map/ppermute | solution.py:28
  68.5 11.8 %collective-permute-start.18 = (bf16[64,2048]{1,0:T(8,128)(2,1)S(1)}, bf16[64,2048]{1,0:T(8,128)(2,1)S(1)}, u32[]{:S(2)}, u32[]{:S(2)}) collective-permute-start(bf16[64,2048]{1,0:T(8,128)(2,1)S(1)} %out_project.11), channel_id=1, source_target_pairs={{0,2},{1,3},{2,4},{3,5},{4,6},{5,7},{6,0},{7,1},{8,10},{9,11},{10,... | collective-permute-start | bytes 786440 | tf_op jit(solution)/shard_map/ppermute | solution.py:33
  74.7 11.2 %collective-permute-start.19 = (bf16[64,2048]{1,0:T(8,128)(2,1)S(1)}, bf16[64,2048]{1,0:T(8,128)(2,1)S(1)}, u32[]{:S(2)}, u32[]{:S(2)}) collective-permute-start(bf16[64,2048]{1,0:T(8,128)(2,1)S(1)} %convert_add_fusion.7), channel_id=1, source_target_pairs={{0,2},{1,3},{2,4},{3,5},{4,6},{5,7},{6,0},{7,1},{8,10},{9,11},{10,... | collective-permute-start | bytes 786440 | tf_op jit(solution)/shard_map/ppermute | solution.py:33
  80.3 11.2 %collective-permute-start.20 = (bf16[64,2048]{1,0:T(8,128)(2,1)S(1)}, bf16[64,2048]{1,0:T(8,128)(2,1)S(1)}, u32[]{:S(2)}, u32[]{:S(2)}) collective-permute-start(bf16[64,2048]{1,0:T(8,128)(2,1)S(1)} %add_convert_fusion.3), channel_id=1, source_target_pairs={{0,2},{1,3},{2,4},{3,5},{4,6},{5,7},{6,0},{7,1},{8,10},{9,11},{10,... | collective-permute-start | bytes 786440 | tf_op jit(solution)/shard_map/ppermute | solution.py:33
  86.0 11.2 %collective-permute-start.21 = (bf16[64,2048]{1,0:T(8,128)(2,1)S(1)}, bf16[64,2048]{1,0:T(8,128)(2,1)S(1)}, u32[]{:S(2)}, u32[]{:S(2)}) collective-permute-start(bf16[64,2048]{1,0:T(8,128)(2,1)S(1)} %convert_add_fusion.6), channel_id=1, source_target_pairs={{0,2},{1,3},{2,4},{3,5},{4,6},{5,7},{6,0},{7,1},{8,10},{9,11},{10,... | collective-permute-start | bytes 786440 | tf_op jit(solution)/shard_map/ppermute | solution.py:33
  102.3 12.8 %collective-permute-start.26 = (bf16[64,2048]{1,0:T(8,128)(2,1)S(1)}, bf16[64,2048]{1,0:T(8,128)(2,1)S(1)}, u32[]{:S(2)}, u32[]{:S(2)}) collective-permute-start(bf16[64,2048]{1,0:T(8,128)(2,1)S(1)} %slice_select_fusion), channel_id=1, source_target_pairs={{0,10},{1,11},{2,12},{3,13},{4,14},{5,15},{6,8},{7,9},{8,18},{9,19... | collective-permute-start | bytes 786440 | tf_op jit(solution)/shard_map/ppermute | solution.py:43
  102.4 17.0 %collective-permute-start.23 = (bf16[64,2048]{1,0:T(8,128)(2,1)S(1)}, bf16[64,2048]{1,0:T(8,128)(2,1)S(1)}, u32[]{:S(2)}, u32[]{:S(2)}) collective-permute-start(bf16[64,2048]{1,0:T(8,128)(2,1)S(1)} %get-tuple-element.102), channel_id=1, source_target_pairs={{0,10},{1,11},{2,12},{3,13},{4,14},{5,15},{6,8},{7,9},{8,18},{9,19... | collective-permute-start | bytes 786440 | tf_op jit(solution)/shard_map/ppermute | solution.py:43
  120.1 12.7 %collective-permute-start.36 = (bf16[64,2048]{1,0:T(8,128)(2,1)S(1)}, bf16[64,2048]{1,0:T(8,128)(2,1)S(1)}, u32[]{:S(2)}, u32[]{:S(2)}) collective-permute-start(bf16[64,2048]{1,0:T(8,128)(2,1)S(1)} %slice_select_fusion), channel_id=1, source_target_pairs={{0,8},{1,9},{2,10},{3,11},{4,12},{5,13},{6,14},{7,15},{8,16},{9,17... | collective-permute-start | bytes 786440 | tf_op jit(solution)/shard_map/ppermute | solution.py:43
  122.5 13.5 %collective-permute-start.24 = (bf16[64,2048]{1,0:T(8,128)(2,1)S(1)}, bf16[64,2048]{1,0:T(8,128)(2,1)S(1)}, u32[]{:S(2)}, u32[]{:S(2)}) collective-permute-start(bf16[64,2048]{1,0:T(8,128)(2,1)S(1)} %collective-permute-done.23.weight.refs_0_), channel_id=1, source_target_pairs={{0,2},{1,3},{2,4},{3,5},{4,6},{5,7},{6,0},{7,1},{8,10},{9,11},{10,... | collective-permute-start | bytes 786440 | tf_op jit(solution)/shard_map/ppermute | solution.py:33
  122.5 13.5 %collective-permute-start.34 = (bf16[64,2048]{1,0:T(8,128)(2,1)S(1)}, bf16[64,2048]{1,0:T(8,128)(2,1)S(1)}, u32[]{:S(2)}, u32[]{:S(2)}) collective-permute-start(bf16[64,2048]{1,0:T(8,128)(2,1)S(1)} %collective-permute-done.26.refs_1_), channel_id=1, source_target_pairs={{0,1},{1,0},{2,3},{3,2},{4,5},{5,4},{6,7},{7,6},{8,9},{9,8},{10,11... | collective-permute-start | bytes 786440 | tf_op jit(solution)/shard_map/ppermute | solution.py:28
  136.0 11.2 %collective-permute-start.33 = (bf16[64,2048]{1,0:T(8,128)(2,1)S(1)}, bf16[64,2048]{1,0:T(8,128)(2,1)S(1)}, u32[]{:S(2)}, u32[]{:S(2)}) collective-permute-start(bf16[64,2048]{1,0:T(8,128)(2,1)S(1)} %collective-permute-done.23.weight.refs_0_), channel_id=1, source_target_pairs={{0,1},{1,0},{2,3},{3,2},{4,5},{5,4},{6,7},{7,6},{8,9},{9,8},{10,11... | collective-permute-start | bytes 786440 | tf_op jit(solution)/shard_map/ppermute | solution.py:28
  164.7 15.1 %collective-permute-start.42 = (bf16[64,2048]{1,0:T(8,128)(2,1)S(1)}, bf16[64,2048]{1,0:T(8,128)(2,1)S(1)}, u32[]{:S(2)}, u32[]{:S(2)}) collective-permute-start(bf16[64,2048]{1,0:T(8,128)(2,1)S(1)} %out_project.16), channel_id=1, source_target_pairs={{0,2},{1,3},{2,4},{3,5},{4,6},{5,7},{6,0},{7,1},{8,10},{9,11},{10,... | collective-permute-start | bytes 786440 | tf_op jit(solution)/shard_map/ppermute | solution.py:33
  174.3 11.2 %collective-permute-start.43 = (bf16[64,2048]{1,0:T(8,128)(2,1)S(1)}, bf16[64,2048]{1,0:T(8,128)(2,1)S(1)}, u32[]{:S(2)}, u32[]{:S(2)}) collective-permute-start(bf16[64,2048]{1,0:T(8,128)(2,1)S(1)} %convert_add_fusion.3), channel_id=1, source_target_pairs={{0,2},{1,3},{2,4},{3,5},{4,6},{5,7},{6,0},{7,1},{8,10},{9,11},{10,... | collective-permute-start | bytes 786440 | tf_op jit(solution)/shard_map/ppermute | solution.py:33
  179.9 11.2 %collective-permute-start.44 = (bf16[64,2048]{1,0:T(8,128)(2,1)S(1)}, bf16[64,2048]{1,0:T(8,128)(2,1)S(1)}, u32[]{:S(2)}, u32[]{:S(2)}) collective-permute-start(bf16[64,2048]{1,0:T(8,128)(2,1)S(1)} %add_convert_fusion.1), channel_id=1, source_target_pairs={{0,2},{1,3},{2,4},{3,5},{4,6},{5,7},{6,0},{7,1},{8,10},{9,11},{10,... | collective-permute-start | bytes 786440 | tf_op jit(solution)/shard_map/ppermute | solution.py:33
  185.5 11.2 %collective-permute-start.45 = (bf16[64,2048]{1,0:T(8,128)(2,1)S(1)}, bf16[64,2048]{1,0:T(8,128)(2,1)S(1)}, u32[]{:S(2)}, u32[]{:S(2)}) collective-permute-start(bf16[64,2048]{1,0:T(8,128)(2,1)S(1)} %convert_add_fusion.2), channel_id=1, source_target_pairs={{0,2},{1,3},{2,4},{3,5},{4,6},{5,7},{6,0},{7,1},{8,10},{9,11},{10,... | collective-permute-start | bytes 786440 | tf_op jit(solution)/shard_map/ppermute | solution.py:33
  (49 other events, 430.1 us)

commit v2 on v1

--- a/solution.py
+++ b/solution.py
@@ -215,8 +215,12 @@
     )(where, *params)
 
 
+LOG2_E = 1.4426950408889634
+
+
 def silu(value):
-    return value / (1.0 + jnp.exp(-value))
+    half = 0.5 * value
+    return half + half * jnp.tanh(half)
 
 
 def split_terms(value, terms):
@@ -267,8 +271,8 @@
         preferred_element_type=f32,
     )
     block_total = cumulus[BLOCK - 1 : BLOCK, :]
-    cumulus_t = cumulus.T
-    step_t = step.T
+    scaled = cumulus * LOG2_E
+    lowered_t = (scaled - jnp.log2(step)).T
     scores = lax.dot_general(c, b, (((1,), (1,)), ((), ())), preferred_element_type=f32)
     spread = spread_of(chans).astype(bf16)
     spread = jnp.concatenate([spread, spread], axis=0)
@@ -297,8 +301,8 @@
         left, right = [], []
         for j in range(QUAD):
             h = quad * QUAD + j
-            gap = jnp.where(lower, cumulus[:, h : h + 1] - cumulus_t[h : h + 1, :], -1e30)
-            left.append((scores * jnp.exp(gap) * step_t[h : h + 1, :]).astype(bf16))
+            gap = jnp.where(lower, scaled[:, h : h + 1] - lowered_t[h : h + 1, :], -1e30)
+            left.append((scores * jnp.exp2(gap)).astype(bf16))
             right.append(jnp.where(lane_head == j, x_quad, jnp.zeros_like(x_quad)))
         diagonal = jnp.dot(
             jnp.concatenate(left, axis=1),
@@ -424,7 +428,11 @@
         return [shard[:, i * piece : (i + 1) * piece] for i in range(PIECES)]
 
     entering = in_pieces(inflow[0])
-    arriving = [chip_ring(x) for x in entering]
+    traded = [swapped(entering[0], 1)]
+    arriving = []
+    for i, x in enumerate(entering):
+        x = after(x, traded) if i else x
+        arriving.append(chip_ring(x))
 
     def regrouped(weight, i):
         rows = slice(i * piece, (i + 1) * piece)
@@ -454,7 +462,8 @@
     )
     out_swapped = swapped(out_weight[0], 1)
 
-    def layer(held, arriving, staged=None):
+    def layer(held, arriving, where_ready, traded=(), staged=None):
+        traded = list(traded)
         buffers = None
         indices = where_ready
         pausing = staged is not None
@@ -467,7 +476,8 @@
                 if pausing:
                     indices = ready(indices, held[0])
                 held = [chip_ring(x) for x in held]
-            other = [swapped(part, 1) for part in held]
+            other = [swapped(part, 1) for part in held[len(traded) :]]
+            other, traded = traded + other, []
             buffers = project(
                 indices, step, chips, held + other, (*xz_parts, p_local), length, buffers
             )
@@ -498,15 +508,16 @@
                 running = [chip_ring(x) for x in parts]
         return parts, staged
 
-    first, staged = layer(entering, arriving)
+    first, staged = layer(entering, arriving, where_ready, traded)
     leaving = []
     for i, new in enumerate(in_pieces(fresh[0])):
         if leaving:
             first[i] = after(first[i], leaving)
         leaving.append(jnp.where(position == sections - 1, new, first[i].astype(bf16)))
     ahead = [next_section(x, 1) for x in leaving]
+    where_later = ready(where_ready, leaving[0])
     level = [next_section(x, 0) for x in after(leaving, ahead)]
-    second, _ = layer(level, ahead, staged)
+    second, _ = layer(level, ahead, where_later, (), staged)
     return jnp.stack([jnp.concatenate(first, axis=1), jnp.concatenate(second, axis=1)])[None]
 
 

time: 204 us -> 204 us (level)
  waiting for transfers between devices: 114 us -> 111 us
  starting transfers between devices: 15 us -> 17.5 us
    ppermute x22, waiting for transfers between devices: 94.6 us -> 88.8 us  [chip_ring(): lax.ppermute(value, 'seq', [(i, (i + 2) % count) for i in range(count)])]
    ppermute x21, waiting for transfers between devices: 1.32 us -> 4.43 us  [swapped(): return lax.ppermute(value, 'seq', [(i, i ^ bit) for i in range(count)])]
    ppermute x22, starting transfers between devices: 6.88 us -> 8.99 us  [chip_ring(): lax.ppermute(value, 'seq', [(i, (i + 2) % count) for i in range(count)])]
    pallas_call x3 -> x4, Pallas kernels: 3.41 us -> 4.55 us  [ready(): pl.pallas_call(ready_kernel, in_specs=[IN_SMEM, pl.BlockSpec(memory_space...]
where the time goes in v2:
time: 204 us
  waiting for transfers between devices  111 us (54%)
  Pallas kernels  55.7 us (27%)
  starting transfers between devices  17.5 us (9%)
  local copies, waits for them, and re-layouts  14.6 us (7%)
  other arithmetic  2.46 us (1%)
    ppermute x22, waiting for transfers between devices, chip_ring(): lax.ppermute(value, 'seq', [(i, (i + 2) % count) for i in range(count)])  88.8 us
    pallas_call x10, Pallas kernels, out_project(): pl.pallas_call(functools.partial(out_kernel, steps=steps, chips=chips, fi...  18.3 us
    pallas_call x8, Pallas kernels, project(): pl.pallas_call(functools.partial(project_kernel, steps=steps, chips=chips...  18 us
    ppermute x4, waiting for transfers between devices, next_section(): return lax.ppermute(value, ('section', 'seq'), pairs)  17.4 us
    pallas_call x2, Pallas kernels, mix(): pl.pallas_call(mix_kernel, grid=(length // BLOCK,), in_specs=[IN_SMEM] +...  11.5 us
    unnamed x50, local copies, waits for them, and re-layouts  9.73 us
    ppermute x22, starting transfers between devices, chip_ring(): lax.ppermute(value, 'seq', [(i, (i + 2) % count) for i in range(count)])  8.99 us
    ppermute x4, starting transfers between devices, next_section(): return lax.ppermute(value, ('section', 'seq'), pairs)  5.02 us
  transfers between devices with their start and end apart: 47, of which 25 were waited for; matrix products, arithmetic and copies ran while one was open for 3% of the time, Pallas kernels for 22%

profile of v2, /device:TPU:0, one launch (start us, length us, event | category | flops | bytes accessed | tf_op | source)
XLA Modules:
  0.0 203.5 jit_solution(12340597112713418993)
XLA Ops:
  1.6 3.1 %collective-permute-start = (bf16[64,2048]{1,0:T(8,128)(2,1)S(1)}, bf16[64,2048]{1,0:T(8,128)(2,1)S(1)}, u32[]{:S(2)}, u32[]{:S(2)}) collective-permute-start(bf16[64,2048]{1,0:T(8,128)(2,1)S(1)} %get-tuple-element.134.refs_0_), channel_id=1, source_target_pairs={{0,2},{1,3},{2,4},{3,5},{4,6},{5,7},{6,0},{7,1},{8,10},{9,11},{10,... | collective-permute-start | bytes 786440 | tf_op jit(solution)/shard_map/ppermute | solution.py:33
  4.7 3.2 %collective-permute-done.3.refs_2_ = bf16[64,2048]{1,0:T(8,128)(2,1)S(1)} collective-permute-done((bf16[64,2048]{1,0:T(8,128)(2,1)S(1)}, bf16[64,2048]{1,0:T(8,128)(2,1)S(1)}, u32[]{:S(2)}, u32[]{:S(2)}) %collective-permute-start.3) | collective-permute-done | bytes 262176 | tf_op jit(solution)/shard_map/ppermute | solution.py:28
  13.3 6.7 %collective-permute-done.4.refs_1_ = bf16[64,2048]{1,0:T(8,128)(2,1)S(1)} collective-permute-done((bf16[64,2048]{1,0:T(8,128)(2,1)S(1)}, bf16[64,2048]{1,0:T(8,128)(2,1)S(1)}, u32[]{:S(2)}, u32[]{:S(2)}) %collective-permute-start.4) | collective-permute-done | bytes 262176 | tf_op jit(solution)/shard_map/ppermute | solution.py:33
  27.3 3.5 %collective-permute-done.5.refs_1_ = bf16[64,2048]{1,0:T(8,128)(2,1)} collective-permute-done((bf16[64,2048]{1,0:T(8,128)(2,1)S(1)}, bf16[64,2048]{1,0:T(8,128)(2,1)}, u32[]{:S(2)}, u32[]{:S(2)}) %collective-permute-start.5) | collective-permute-done | bytes 262176 | tf_op jit(solution)/shard_map/ppermute | solution.py:33
  38.3 4.1 %collective-permute-done.6.refs_1_ = bf16[64,2048]{1,0:T(8,128)(2,1)S(1)} collective-permute-done((bf16[64,2048]{1,0:T(8,128)(2,1)}, bf16[64,2048]{1,0:T(8,128)(2,1)S(1)}, u32[]{:S(2)}, u32[]{:S(2)}) %collective-permute-start.6) | collective-permute-done | bytes 262176 | tf_op jit(solution)/shard_map/ppermute | solution.py:33
  51.8 5.8 %mix.2 = (bf16[256,512]{1,0:T(8,128)(2,1)S(1)}, bf16[256,512]{1,0:T(8,128)(2,1)S(1)}, f32[256,128]{1,0:T(8,128)S(1)}, f32[256,128]{1,0:T(8,128)S(1)}) custom-call(s32[2]{0:T(128)S(1)} %pad_add_fusion.where, bf16[512,1024]{1,0:T(8,128)(2,1)S(1)} %get-tuple-element.77.xz_ref, bf16[512,256]{1,0:T(8,128)(2,1)S(1)} %get-tuple-element.78.p_ref, ...), custom_call_target="tpu_custom_call" | custom-call | flops 536870912 | bytes 1835008 | tf_op jit(solution)/shard_map/mix/pallas_call | solution.py:332
  64.0 3.4 %copy-done.1 = bf16[1024,4096]{1,0:T(8,128)(2,1)S(1)} copy-done((bf16[1024,4096]{1,0:T(8,128)(2,1)S(1)}, bf16[1024,4096]{1,0:T(8,128)(2,1)}, u32[]{:S(2)}) %copy-start.1) | copy-done | bytes 8388632
  75.1 5.5 %collective-permute-done.18 = bf16[64,2048]{1,0:T(8,128)(2,1)S(1)} collective-permute-done((bf16[64,2048]{1,0:T(8,128)(2,1)S(1)}, bf16[64,2048]{1,0:T(8,128)(2,1)S(1)}, u32[]{:S(2)}, u32[]{:S(2)}) %collective-permute-start.18) | collective-permute-done | bytes 262176 | tf_op jit(solution)/shard_map/ppermute | solution.py:33
  82.9 3.3 %collective-permute-done.19 = bf16[64,2048]{1,0:T(8,128)(2,1)S(1)} collective-permute-done((bf16[64,2048]{1,0:T(8,128)(2,1)S(1)}, bf16[64,2048]{1,0:T(8,128)(2,1)S(1)}, u32[]{:S(2)}, u32[]{:S(2)}) %collective-permute-start.19) | collective-permute-done | bytes 262176 | tf_op jit(solution)/shard_map/ppermute | solution.py:33
  86.4 5.5 %collective-permute-done.20 = bf16[64,2048]{1,0:T(8,128)(2,1)S(1)} collective-permute-done((bf16[64,2048]{1,0:T(8,128)(2,1)S(1)}, bf16[64,2048]{1,0:T(8,128)(2,1)S(1)}, u32[]{:S(2)}, u32[]{:S(2)}) %collective-permute-start.20) | collective-permute-done | bytes 262176 | tf_op jit(solution)/shard_map/ppermute | solution.py:33
  94.2 3.3 %collective-permute-done.21 = bf16[64,2048]{1,0:T(8,128)(2,1)S(1)} collective-permute-done((bf16[64,2048]{1,0:T(8,128)(2,1)S(1)}, bf16[64,2048]{1,0:T(8,128)(2,1)S(1)}, u32[]{:S(2)}, u32[]{:S(2)}) %collective-permute-start.21) | collective-permute-done | bytes 262176 | tf_op jit(solution)/shard_map/ppermute | solution.py:33
  97.6 5.0 %collective-permute-done.22 = bf16[64,2048]{1,0:T(8,128)(2,1)S(1)} collective-permute-done((bf16[64,2048]{1,0:T(8,128)(2,1)S(1)}, bf16[64,2048]{1,0:T(8,128)(2,1)S(1)}, u32[]{:S(2)}, u32[]{:S(2)}) %collective-permute-start.22) | collective-permute-done | bytes 262176 | tf_op jit(solution)/shard_map/ppermute | solution.py:33
  104.8 10.7 %collective-permute-done.26.refs_1_ = bf16[64,2048]{1,0:T(8,128)(2,1)S(1)} collective-permute-done((bf16[64,2048]{1,0:T(8,128)(2,1)S(1)}, bf16[64,2048]{1,0:T(8,128)(2,1)S(1)}, u32[]{:S(2)}, u32[]{:S(2)}) %collective-permute-start.26) | collective-permute-done | bytes 262176 | tf_op jit(solution)/shard_map/ppermute | solution.py:43
  115.5 4.2 %collective-permute-done.23.weight.refs_0_ = bf16[64,2048]{1,0:T(8,128)(2,1)S(1)} collective-permute-done((bf16[64,2048]{1,0:T(8,128)(2,1)S(1)}, bf16[64,2048]{1,0:T(8,128)(2,1)S(1)}, u32[]{:S(2)}, u32[]{:S(2)}) %collective-permute-start.23) | collective-permute-done | bytes 262176 | tf_op jit(solution)/shard_map/ppermute | solution.py:43
  122.7 8.0 %collective-permute-done.27.refs_1_ = bf16[64,2048]{1,0:T(8,128)(2,1)S(1)} collective-permute-done((bf16[64,2048]{1,0:T(8,128)(2,1)S(1)}, bf16[64,2048]{1,0:T(8,128)(2,1)S(1)}, u32[]{:S(2)}, u32[]{:S(2)}) %collective-permute-start.27) | collective-permute-done | bytes 262176 | tf_op jit(solution)/shard_map/ppermute | solution.py:33
  133.2 3.1 %collective-permute-done.24.weight.refs_0_ = bf16[64,2048]{1,0:T(8,128)(2,1)S(1)} collective-permute-done((bf16[64,2048]{1,0:T(8,128)(2,1)S(1)}, bf16[64,2048]{1,0:T(8,128)(2,1)S(1)}, u32[]{:S(2)}, u32[]{:S(2)}) %collective-permute-start.24) | collective-permute-done | bytes 262176 | tf_op jit(solution)/shard_map/ppermute | solution.py:33
  136.3 5.0 %collective-permute-done.28.refs_1_ = bf16[64,2048]{1,0:T(8,128)(2,1)S(1)} collective-permute-done((bf16[64,2048]{1,0:T(8,128)(2,1)S(1)}, bf16[64,2048]{1,0:T(8,128)(2,1)S(1)}, u32[]{:S(2)}, u32[]{:S(2)}) %collective-permute-start.28) | collective-permute-done | bytes 262176 | tf_op jit(solution)/shard_map/ppermute | solution.py:33
  154.7 5.8 %mix.3 = (bf16[256,512]{1,0:T(8,128)(2,1)S(1)}, bf16[256,512]{1,0:T(8,128)(2,1)S(1)}, f32[256,128]{1,0:T(8,128)S(1)}, f32[256,128]{1,0:T(8,128)S(1)}) custom-call(s32[2]{0:T(128)S(1)} %pad_add_fusion.where, bf16[512,1024]{1,0:T(8,128)(2,1)S(1)} %get-tuple-element.112.xz_ref, bf16[512,256]{1,0:T(8,128)(2,1)S(1)} %get-tuple-element.113.p_ref, ...), custom_call_target="tpu_custom_call" | custom-call | flops 536870912 | bytes 1835008 | tf_op jit(solution)/shard_map/mix/pallas_call | solution.py:332
  167.3 7.3 %collective-permute-done.41 = bf16[64,2048]{1,0:T(8,128)(2,1)S(1)} collective-permute-done((bf16[64,2048]{1,0:T(8,128)(2,1)S(1)}, bf16[64,2048]{1,0:T(8,128)(2,1)S(1)}, u32[]{:S(2)}, u32[]{:S(2)}) %collective-permute-start.41) | collective-permute-done | bytes 262176 | tf_op jit(solution)/shard_map/ppermute | solution.py:33
  174.8 5.5 %collective-permute-done.42 = bf16[64,2048]{1,0:T(8,128)(2,1)S(1)} collective-permute-done((bf16[64,2048]{1,0:T(8,128)(2,1)S(1)}, bf16[64,2048]{1,0:T(8,128)(2,1)S(1)}, u32[]{:S(2)}, u32[]{:S(2)}) %collective-permute-start.42) | collective-permute-done | bytes 262176 | tf_op jit(solution)/shard_map/ppermute | solution.py:33
  182.5 3.4 %collective-permute-done.43 = bf16[64,2048]{1,0:T(8,128)(2,1)S(1)} collective-permute-done((bf16[64,2048]{1,0:T(8,128)(2,1)S(1)}, bf16[64,2048]{1,0:T(8,128)(2,1)S(1)}, u32[]{:S(2)}, u32[]{:S(2)}) %collective-permute-start.43) | collective-permute-done | bytes 262176 | tf_op jit(solution)/shard_map/ppermute | solution.py:33
  186.0 5.5 %collective-permute-done.44 = bf16[64,2048]{1,0:T(8,128)(2,1)S(1)} collective-permute-done((bf16[64,2048]{1,0:T(8,128)(2,1)S(1)}, bf16[64,2048]{1,0:T(8,128)(2,1)S(1)}, u32[]{:S(2)}, u32[]{:S(2)}) %collective-permute-start.44) | collective-permute-done | bytes 262176 | tf_op jit(solution)/shard_map/ppermute | solution.py:33
  193.7 3.4 %collective-permute-done.45 = bf16[64,2048]{1,0:T(8,128)(2,1)S(1)} collective-permute-done((bf16[64,2048]{1,0:T(8,128)(2,1)S(1)}, bf16[64,2048]{1,0:T(8,128)(2,1)S(1)}, u32[]{:S(2)}, u32[]{:S(2)}) %collective-permute-start.45) | collective-permute-done | bytes 262176 | tf_op jit(solution)/shard_map/ppermute | solution.py:33
  197.2 4.7 %collective-permute-done.46 = bf16[64,2048]{1,0:T(8,128)(2,1)S(1)} collective-permute-done((bf16[64,2048]{1,0:T(8,128)(2,1)S(1)}, bf16[64,2048]{1,0:T(8,128)(2,1)S(1)}, u32[]{:S(2)}, u32[]{:S(2)}) %collective-permute-start.46) | collective-permute-done | bytes 262176 | tf_op jit(solution)/shard_map/ppermute | solution.py:33
  (175 shorter events, 83.9 us)
Async XLA Ops:
  0.0 58.2 %collective-permute-start.15 = (bf16[512,4096]{1,0:T(8,128)(2,1)}, bf16[512,4096]{1,0:T(8,128)(2,1)}, u32[]{:S(2)}, u32[]{:S(2)}) collective-permute-start(bf16[512,4096]{1,0:T(8,128)(2,1)} %bitcast.39), channel_id=1, source_target_pairs={{0,1},{1,0},{2,3},{3,2},{4,5},{5,4},{6,7},{7,6},{8,9},{9,8},{10,11... | collective-permute-start | bytes 12582920 | tf_op jit(solution)/shard_map/ppermute | solution.py:28
  1.6 11.6 %collective-permute-start = (bf16[64,2048]{1,0:T(8,128)(2,1)S(1)}, bf16[64,2048]{1,0:T(8,128)(2,1)S(1)}, u32[]{:S(2)}, u32[]{:S(2)}) collective-permute-start(bf16[64,2048]{1,0:T(8,128)(2,1)S(1)} %get-tuple-element.134.refs_0_), channel_id=1, source_target_pairs={{0,2},{1,3},{2,4},{3,5},{4,6},{5,7},{6,0},{7,1},{8,10},{9,11},{10,... | collective-permute-start | bytes 786440 | tf_op jit(solution)/shard_map/ppermute | solution.py:33
  7.9 12.1 %collective-permute-start.4 = (bf16[64,2048]{1,0:T(8,128)(2,1)S(1)}, bf16[64,2048]{1,0:T(8,128)(2,1)S(1)}, u32[]{:S(2)}, u32[]{:S(2)}) collective-permute-start(bf16[64,2048]{1,0:T(8,128)(2,1)S(1)} %get-tuple-element.68.refs_1_), channel_id=1, source_target_pairs={{0,2},{1,3},{2,4},{3,5},{4,6},{5,7},{6,0},{7,1},{8,10},{9,11},{10,... | collective-permute-start | bytes 786440 | tf_op jit(solution)/shard_map/ppermute | solution.py:33
  13.3 12.1 %collective-permute-start.11 = (bf16[64,2048]{1,0:T(8,128)(2,1)S(1)}, bf16[64,2048]{1,0:T(8,128)(2,1)S(1)}, u32[]{:S(2)}, u32[]{:S(2)}) collective-permute-start(bf16[64,2048]{1,0:T(8,128)(2,1)S(1)} %collective-permute-done.refs_0_), channel_id=1, source_target_pairs={{0,1},{1,0},{2,3},{3,2},{4,5},{5,4},{6,7},{7,6},{8,9},{9,8},{10,11... | collective-permute-start | bytes 786440 | tf_op jit(solution)/shard_map/ppermute | solution.py:28
  13.3 12.0 %collective-permute-start.1 = (bf16[64,2048]{1,0:T(8,128)(2,1)S(1)}, bf16[64,2048]{1,0:T(8,128)(2,1)}, u32[]{:S(2)}, u32[]{:S(2)}) collective-permute-start(bf16[64,2048]{1,0:T(8,128)(2,1)S(1)} %collective-permute-done.refs_0_), channel_id=1, source_target_pairs={{0,2},{1,3},{2,4},{3,5},{4,6},{5,7},{6,0},{7,1},{8,10},{9,11},{10,... | collective-permute-start | bytes 786440 | tf_op jit(solution)/shard_map/ppermute | solution.py:33
  25.3 21.5 %collective-permute-start.9 = (bf16[64,2048]{1,0:T(8,128)(2,1)}, bf16[64,2048]{1,0:T(8,128)(2,1)S(1)}, u32[]{:S(2)}, u32[]{:S(2)}) collective-permute-start(bf16[64,2048]{1,0:T(8,128)(2,1)} %collective-permute-done.1.refs_0_), channel_id=1, source_target_pairs={{0,1},{1,0},{2,3},{3,2},{4,5},{5,4},{6,7},{7,6},{8,9},{9,8},{10,11... | collective-permute-start | bytes 786440 | tf_op jit(solution)/shard_map/ppermute | solution.py:28
  26.0 11.7 %collective-permute-start.2 = (bf16[64,2048]{1,0:T(8,128)(2,1)}, bf16[64,2048]{1,0:T(8,128)(2,1)S(1)}, u32[]{:S(2)}, u32[]{:S(2)}) collective-permute-start(bf16[64,2048]{1,0:T(8,128)(2,1)} %collective-permute-done.1.refs_0_), channel_id=1, source_target_pairs={{0,2},{1,3},{2,4},{3,5},{4,6},{5,7},{6,0},{7,1},{8,10},{9,11},{10,... | collective-permute-start | bytes 786440 | tf_op jit(solution)/shard_map/ppermute | solution.py:33
  30.8 16.1 %collective-permute-start.10 = (bf16[64,2048]{1,0:T(8,128)(2,1)}, bf16[64,2048]{1,0:T(8,128)(2,1)S(1)}, u32[]{:S(2)}, u32[]{:S(2)}) collective-permute-start(bf16[64,2048]{1,0:T(8,128)(2,1)} %collective-permute-done.5.refs_1_), channel_id=1, source_target_pairs={{0,1},{1,0},{2,3},{3,2},{4,5},{5,4},{6,7},{7,6},{8,9},{9,8},{10,11... | collective-permute-start | bytes 786440 | tf_op jit(solution)/shard_map/ppermute | solution.py:28
  37.7 11.8 %collective-permute-start.7 = (bf16[64,2048]{1,0:T(8,128)(2,1)S(1)}, bf16[64,2048]{1,0:T(8,128)(2,1)S(1)}, u32[]{:S(2)}, u32[]{:S(2)}) collective-permute-start(bf16[64,2048]{1,0:T(8,128)(2,1)S(1)} %collective-permute-done.2.refs_0_), channel_id=1, source_target_pairs={{0,1},{1,0},{2,3},{3,2},{4,5},{5,4},{6,7},{7,6},{8,9},{9,8},{10,11... | collective-permute-start | bytes 786440 | tf_op jit(solution)/shard_map/ppermute | solution.py:28
  68.8 11.8 %collective-permute-start.18 = (bf16[64,2048]{1,0:T(8,128)(2,1)S(1)}, bf16[64,2048]{1,0:T(8,128)(2,1)S(1)}, u32[]{:S(2)}, u32[]{:S(2)}) collective-permute-start(bf16[64,2048]{1,0:T(8,128)(2,1)S(1)} %out_project.11), channel_id=1, source_target_pairs={{0,2},{1,3},{2,4},{3,5},{4,6},{5,7},{6,0},{7,1},{8,10},{9,11},{10,... | collective-permute-start | bytes 786440 | tf_op jit(solution)/shard_map/ppermute | solution.py:33
  75.1 11.2 %collective-permute-start.19 = (bf16[64,2048]{1,0:T(8,128)(2,1)S(1)}, bf16[64,2048]{1,0:T(8,128)(2,1)S(1)}, u32[]{:S(2)}, u32[]{:S(2)}) collective-permute-start(bf16[64,2048]{1,0:T(8,128)(2,1)S(1)} %convert_add_fusion.7), channel_id=1, source_target_pairs={{0,2},{1,3},{2,4},{3,5},{4,6},{5,7},{6,0},{7,1},{8,10},{9,11},{10,... | collective-permute-start | bytes 786440 | tf_op jit(solution)/shard_map/ppermute | solution.py:33
  80.7 11.2 %collective-permute-start.20 = (bf16[64,2048]{1,0:T(8,128)(2,1)S(1)}, bf16[64,2048]{1,0:T(8,128)(2,1)S(1)}, u32[]{:S(2)}, u32[]{:S(2)}) collective-permute-start(bf16[64,2048]{1,0:T(8,128)(2,1)S(1)} %add_convert_fusion.3), channel_id=1, source_target_pairs={{0,2},{1,3},{2,4},{3,5},{4,6},{5,7},{6,0},{7,1},{8,10},{9,11},{10,... | collective-permute-start | bytes 786440 | tf_op jit(solution)/shard_map/ppermute | solution.py:33
  86.3 11.2 %collective-permute-start.21 = (bf16[64,2048]{1,0:T(8,128)(2,1)S(1)}, bf16[64,2048]{1,0:T(8,128)(2,1)S(1)}, u32[]{:S(2)}, u32[]{:S(2)}) collective-permute-start(bf16[64,2048]{1,0:T(8,128)(2,1)S(1)} %convert_add_fusion.6), channel_id=1, source_target_pairs={{0,2},{1,3},{2,4},{3,5},{4,6},{5,7},{6,0},{7,1},{8,10},{9,11},{10,... | collective-permute-start | bytes 786440 | tf_op jit(solution)/shard_map/ppermute | solution.py:33
  102.7 12.8 %collective-permute-start.26 = (bf16[64,2048]{1,0:T(8,128)(2,1)S(1)}, bf16[64,2048]{1,0:T(8,128)(2,1)S(1)}, u32[]{:S(2)}, u32[]{:S(2)}) collective-permute-start(bf16[64,2048]{1,0:T(8,128)(2,1)S(1)} %slice_select_fusion), channel_id=1, source_target_pairs={{0,10},{1,11},{2,12},{3,13},{4,14},{5,15},{6,8},{7,9},{8,18},{9,19... | collective-permute-start | bytes 786440 | tf_op jit(solution)/shard_map/ppermute | solution.py:43
  102.7 17.0 %collective-permute-start.23 = (bf16[64,2048]{1,0:T(8,128)(2,1)S(1)}, bf16[64,2048]{1,0:T(8,128)(2,1)S(1)}, u32[]{:S(2)}, u32[]{:S(2)}) collective-permute-start(bf16[64,2048]{1,0:T(8,128)(2,1)S(1)} %get-tuple-element.104.weight), channel_id=1, source_target_pairs={{0,10},{1,11},{2,12},{3,13},{4,14},{5,15},{6,8},{7,9},{8,18},{9,19... | collective-permute-start | bytes 786440 | tf_op jit(solution)/shard_map/ppermute | solution.py:43
  120.3 12.9 %collective-permute-start.36 = (bf16[64,2048]{1,0:T(8,128)(2,1)S(1)}, bf16[64,2048]{1,0:T(8,128)(2,1)S(1)}, u32[]{:S(2)}, u32[]{:S(2)}) collective-permute-start(bf16[64,2048]{1,0:T(8,128)(2,1)S(1)} %slice_select_fusion), channel_id=1, source_target_pairs={{0,8},{1,9},{2,10},{3,11},{4,12},{5,13},{6,14},{7,15},{8,16},{9,17... | collective-permute-start | bytes 786440 | tf_op jit(solution)/shard_map/ppermute | solution.py:43
  122.6 13.7 %collective-permute-start.24 = (bf16[64,2048]{1,0:T(8,128)(2,1)S(1)}, bf16[64,2048]{1,0:T(8,128)(2,1)S(1)}, u32[]{:S(2)}, u32[]{:S(2)}) collective-permute-start(bf16[64,2048]{1,0:T(8,128)(2,1)S(1)} %collective-permute-done.23.weight.refs_0_), channel_id=1, source_target_pairs={{0,2},{1,3},{2,4},{3,5},{4,6},{5,7},{6,0},{7,1},{8,10},{9,11},{10,... | collective-permute-start | bytes 786440 | tf_op jit(solution)/shard_map/ppermute | solution.py:33
  122.6 13.7 %collective-permute-start.34 = (bf16[64,2048]{1,0:T(8,128)(2,1)S(1)}, bf16[64,2048]{1,0:T(8,128)(2,1)S(1)}, u32[]{:S(2)}, u32[]{:S(2)}) collective-permute-start(bf16[64,2048]{1,0:T(8,128)(2,1)S(1)} %collective-permute-done.26.refs_1_), channel_id=1, source_target_pairs={{0,1},{1,0},{2,3},{3,2},{4,5},{5,4},{6,7},{7,6},{8,9},{9,8},{10,11... | collective-permute-start | bytes 786440 | tf_op jit(solution)/shard_map/ppermute | solution.py:28
  133.2 12.1 %collective-permute-start.38 = (bf16[64,2048]{1,0:T(8,128)(2,1)S(1)}, bf16[64,2048]{1,0:T(8,128)(2,1)S(1)}, u32[]{:S(2)}, u32[]{:S(2)}) collective-permute-start(bf16[64,2048]{1,0:T(8,128)(2,1)S(1)} %collective-permute-done.36.refs_1_), channel_id=1, source_target_pairs={{0,1},{1,0},{2,3},{3,2},{4,5},{5,4},{6,7},{7,6},{8,9},{9,8},{10,11... | collective-permute-start | bytes 786440 | tf_op jit(solution)/shard_map/ppermute | solution.py:28
  136.3 11.7 %collective-permute-start.33 = (bf16[64,2048]{1,0:T(8,128)(2,1)S(1)}, bf16[64,2048]{1,0:T(8,128)(2,1)S(1)}, u32[]{:S(2)}, u32[]{:S(2)}) collective-permute-start(bf16[64,2048]{1,0:T(8,128)(2,1)S(1)} %collective-permute-done.23.weight.refs_0_), channel_id=1, source_target_pairs={{0,1},{1,0},{2,3},{3,2},{4,5},{5,4},{6,7},{7,6},{8,9},{9,8},{10,11... | collective-permute-start | bytes 786440 | tf_op jit(solution)/shard_map/ppermute | solution.py:28
  165.2 15.1 %collective-permute-start.42 = (bf16[64,2048]{1,0:T(8,128)(2,1)S(1)}, bf16[64,2048]{1,0:T(8,128)(2,1)S(1)}, u32[]{:S(2)}, u32[]{:S(2)}) collective-permute-start(bf16[64,2048]{1,0:T(8,128)(2,1)S(1)} %out_project.16), channel_id=1, source_target_pairs={{0,2},{1,3},{2,4},{3,5},{4,6},{5,7},{6,0},{7,1},{8,10},{9,11},{10,... | collective-permute-start | bytes 786440 | tf_op jit(solution)/shard_map/ppermute | solution.py:33
  174.7 11.2 %collective-permute-start.43 = (bf16[64,2048]{1,0:T(8,128)(2,1)S(1)}, bf16[64,2048]{1,0:T(8,128)(2,1)S(1)}, u32[]{:S(2)}, u32[]{:S(2)}) collective-permute-start(bf16[64,2048]{1,0:T(8,128)(2,1)S(1)} %convert_add_fusion.3), channel_id=1, source_target_pairs={{0,2},{1,3},{2,4},{3,5},{4,6},{5,7},{6,0},{7,1},{8,10},{9,11},{10,... | collective-permute-start | bytes 786440 | tf_op jit(solution)/shard_map/ppermute | solution.py:33
  180.3 11.2 %collective-permute-start.44 = (bf16[64,2048]{1,0:T(8,128)(2,1)S(1)}, bf16[64,2048]{1,0:T(8,128)(2,1)S(1)}, u32[]{:S(2)}, u32[]{:S(2)}) collective-permute-start(bf16[64,2048]{1,0:T(8,128)(2,1)S(1)} %add_convert_fusion.1), channel_id=1, source_target_pairs={{0,2},{1,3},{2,4},{3,5},{4,6},{5,7},{6,0},{7,1},{8,10},{9,11},{10,... | collective-permute-start | bytes 786440 | tf_op jit(solution)/shard_map/ppermute | solution.py:33
  186.0 11.2 %collective-permute-start.45 = (bf16[64,2048]{1,0:T(8,128)(2,1)S(1)}, bf16[64,2048]{1,0:T(8,128)(2,1)S(1)}, u32[]{:S(2)}, u32[]{:S(2)}) collective-permute-start(bf16[64,2048]{1,0:T(8,128)(2,1)S(1)} %convert_add_fusion.2), channel_id=1, source_target_pairs={{0,2},{1,3},{2,4},{3,5},{4,6},{5,7},{6,0},{7,1},{8,10},{9,11},{10,... | collective-permute-start | bytes 786440 | tf_op jit(solution)/shard_map/ppermute | solution.py:33
  (49 other events, 424.3 us)

commit v3 on v2

--- a/solution.py
+++ b/solution.py
@@ -215,9 +215,6 @@
     )(where, *params)
 
 
-LOG2_E = 1.4426950408889634
-
-
 def silu(value):
     half = 0.5 * value
     return half + half * jnp.tanh(half)
@@ -234,25 +231,30 @@
 def mix_kernel(
     where, xz_ref, p_ref, taps_ref, offset_ref, bias_ref, rate_ref, skip_ref, gain_ref,
     mine_ref, theirs_ref, mine_squares, theirs_squares,
-    padded_ref, state_ref, gated_ref, squares_ref,
+    tail_ref, state_ref, gated_ref, squares_ref,
 ):
     chans = mine_ref.shape[1]
     heads = chans // HEAD_DIM
-    lead = 8
     rows = pl.ds(pl.multiple_of(pl.program_id(0) * BLOCK, BLOCK), BLOCK)
 
     @pl.when(pl.program_id(0) == 0)
     def _():
-        padded_ref[0:lead, :] = jnp.zeros((lead, padded_ref.shape[1]), f32)
+        tail_ref[...] = jnp.zeros_like(tail_ref)
         state_ref[...] = jnp.zeros_like(state_ref)
 
-    padded_ref[lead : lead + BLOCK, 0:chans] = xz_ref[rows, chans:].astype(f32)
-    padded_ref[lead : lead + BLOCK, chans:] = p_ref[rows, 0 : 2 * STATE].astype(f32)
-    total = offset_ref[0:1, :]
-    for k in range(CONV):
-        start = lead - (CONV - 1) + k
-        total = total + taps_ref[k : k + 1, :] * padded_ref[start : start + BLOCK, :]
-    padded_ref[0:lead, :] = padded_ref[BLOCK : BLOCK + lead, :]
+    joined = jnp.concatenate(
+        [xz_ref[rows, chans:].astype(f32), p_ref[rows, 0 : 2 * STATE].astype(f32)], axis=1
+    )
+    lead = tail_ref.shape[0]
+    tail = tail_ref[...]
+    top = lax.broadcasted_iota(jnp.int32, tail.shape, 0)
+    total = offset_ref[0:1, :] + taps_ref[CONV - 1 : CONV, :] * joined
+    for back in range(1, CONV):
+        rolled = pltpu.roll(joined, back, 0)
+        first = jnp.where(top < back, pltpu.roll(tail, back, 0), rolled[:lead])
+        moved = jnp.concatenate([first, rolled[lead:]], axis=0)
+        total = total + taps_ref[CONV - 1 - back : CONV - back, :] * moved
+    tail_ref[...] = joined[BLOCK - lead :]
     convolved = silu(total).astype(bf16)
     x = convolved[:, :chans]
     bc = convolved[:, chans:]
@@ -271,8 +273,7 @@
         preferred_element_type=f32,
     )
     block_total = cumulus[BLOCK - 1 : BLOCK, :]
-    scaled = cumulus * LOG2_E
-    lowered_t = (scaled - jnp.log2(step)).T
+    lowered_t = (cumulus - jnp.log(step)).T
     scores = lax.dot_general(c, b, (((1,), (1,)), ((), ())), preferred_element_type=f32)
     spread = spread_of(chans).astype(bf16)
     spread = jnp.concatenate([spread, spread], axis=0)
@@ -301,8 +302,8 @@
         left, right = [], []
         for j in range(QUAD):
             h = quad * QUAD + j
-            gap = jnp.where(lower, scaled[:, h : h + 1] - lowered_t[h : h + 1, :], -1e30)
-            left.append((scores * jnp.exp2(gap)).astype(bf16))
+            gap = jnp.where(lower, cumulus[:, h : h + 1] - lowered_t[h : h + 1, :], -1e30)
+            left.append((scores * jnp.exp(gap)).astype(bf16))
             right.append(jnp.where(lane_head == j, x_quad, jnp.zeros_like(x_quad)))
         diagonal = jnp.dot(
             jnp.concatenate(left, axis=1),
@@ -338,7 +339,7 @@
         out_shape=[jax.ShapeDtypeStruct((length // 2, chans), bf16)] * 2
         + [jax.ShapeDtypeStruct((length // 2, LANES), f32)] * 2,
         scratch_shapes=[
-            pltpu.VMEM((BLOCK + 8, chans + 2 * STATE), f32),
+            pltpu.VMEM((8, chans + 2 * STATE), f32),
             pltpu.VMEM((STATE, chans), f32),
             pltpu.VMEM((BLOCK, chans), bf16),
             pltpu.VMEM((BLOCK, LANES), f32),

time: 204 us -> 202 us (level)
  no operation moved by 1% of the time
where the time goes in v3:
time: 202 us
  waiting for transfers between devices  111 us (55%)
  Pallas kernels  54.3 us (27%)
  starting transfers between devices  17.5 us (9%)
  local copies, waits for them, and re-layouts  14.6 us (7%)
  other arithmetic  2.46 us (1%)
    ppermute x22, waiting for transfers between devices, chip_ring(): lax.ppermute(value, 'seq', [(i, (i + 2) % count) for i in range(count)])  88.8 us
    pallas_call x10, Pallas kernels, out_project(): pl.pallas_call(functools.partial(out_kernel, steps=steps, chips=chips, fi...  18.3 us
    pallas_call x8, Pallas kernels, project(): pl.pallas_call(functools.partial(project_kernel, steps=steps, chips=chips...  18 us
    ppermute x4, waiting for transfers between devices, next_section(): return lax.ppermute(value, ('section', 'seq'), pairs)  17.4 us
    pallas_call x2, Pallas kernels, mix(): pl.pallas_call(mix_kernel, grid=(length // BLOCK,), in_specs=[IN_SMEM] +...  10.2 us
    unnamed x50, local copies, waits for them, and re-layouts  9.73 us
    ppermute x22, starting transfers between devices, chip_ring(): lax.ppermute(value, 'seq', [(i, (i + 2) % count) for i in range(count)])  8.99 us
    ppermute x4, starting transfers between devices, next_section(): return lax.ppermute(value, ('section', 'seq'), pairs)  5.03 us
  transfers between devices with their start and end apart: 47, of which 25 were waited for; matrix products, arithmetic and copies ran while one was open for 3% of the time, Pallas kernels for 22%

profile of v3, /device:TPU:0, one launch (start us, length us, event | category | flops | bytes accessed | tf_op | source)
XLA Modules:
  0.0 202.2 jit_solution(3436535640530364933)
XLA Ops:
  1.6 3.1 %collective-permute-start = (bf16[64,2048]{1,0:T(8,128)(2,1)S(1)}, bf16[64,2048]{1,0:T(8,128)(2,1)S(1)}, u32[]{:S(2)}, u32[]{:S(2)}) collective-permute-start(bf16[64,2048]{1,0:T(8,128)(2,1)S(1)} %get-tuple-element.134.refs_0_), channel_id=1, source_target_pairs={{0,2},{1,3},{2,4},{3,5},{4,6},{5,7},{6,0},{7,1},{8,10},{9,11},{10,... | collective-permute-start | bytes 786440 | tf_op jit(solution)/shard_map/ppermute | solution.py:33
  4.7 3.2 %collective-permute-done.3.refs_2_ = bf16[64,2048]{1,0:T(8,128)(2,1)S(1)} collective-permute-done((bf16[64,2048]{1,0:T(8,128)(2,1)S(1)}, bf16[64,2048]{1,0:T(8,128)(2,1)S(1)}, u32[]{:S(2)}, u32[]{:S(2)}) %collective-permute-start.3) | collective-permute-done | bytes 262176 | tf_op jit(solution)/shard_map/ppermute | solution.py:28
  13.3 6.7 %collective-permute-done.4.refs_1_ = bf16[64,2048]{1,0:T(8,128)(2,1)S(1)} collective-permute-done((bf16[64,2048]{1,0:T(8,128)(2,1)S(1)}, bf16[64,2048]{1,0:T(8,128)(2,1)S(1)}, u32[]{:S(2)}, u32[]{:S(2)}) %collective-permute-start.4) | collective-permute-done | bytes 262176 | tf_op jit(solution)/shard_map/ppermute | solution.py:33
  27.3 3.5 %collective-permute-done.5.refs_1_ = bf16[64,2048]{1,0:T(8,128)(2,1)} collective-permute-done((bf16[64,2048]{1,0:T(8,128)(2,1)S(1)}, bf16[64,2048]{1,0:T(8,128)(2,1)}, u32[]{:S(2)}, u32[]{:S(2)}) %collective-permute-start.5) | collective-permute-done | bytes 262176 | tf_op jit(solution)/shard_map/ppermute | solution.py:33
  38.3 4.1 %collective-permute-done.6.refs_1_ = bf16[64,2048]{1,0:T(8,128)(2,1)S(1)} collective-permute-done((bf16[64,2048]{1,0:T(8,128)(2,1)}, bf16[64,2048]{1,0:T(8,128)(2,1)S(1)}, u32[]{:S(2)}, u32[]{:S(2)}) %collective-permute-start.6) | collective-permute-done | bytes 262176 | tf_op jit(solution)/shard_map/ppermute | solution.py:33
  51.8 5.1 %mix.2 = (bf16[256,512]{1,0:T(8,128)(2,1)S(1)}, bf16[256,512]{1,0:T(8,128)(2,1)S(1)}, f32[256,128]{1,0:T(8,128)S(1)}, f32[256,128]{1,0:T(8,128)S(1)}) custom-call(s32[2]{0:T(128)S(1)} %pad_add_fusion.where, bf16[512,1024]{1,0:T(8,128)(2,1)S(1)} %get-tuple-element.77.xz_ref, bf16[512,256]{1,0:T(8,128)(2,1)S(1)} %get-tuple-element.78.p_ref, ...), custom_call_target="tpu_custom_call" | custom-call | flops 536870912 | bytes 1835008 | tf_op jit(solution)/shard_map/mix/pallas_call | solution.py:333
  63.3 3.4 %copy-done.1 = bf16[1024,4096]{1,0:T(8,128)(2,1)S(1)} copy-done((bf16[1024,4096]{1,0:T(8,128)(2,1)S(1)}, bf16[1024,4096]{1,0:T(8,128)(2,1)}, u32[]{:S(2)}) %copy-start.1) | copy-done | bytes 8388632
  74.5 5.5 %collective-permute-done.18 = bf16[64,2048]{1,0:T(8,128)(2,1)S(1)} collective-permute-done((bf16[64,2048]{1,0:T(8,128)(2,1)S(1)}, bf16[64,2048]{1,0:T(8,128)(2,1)S(1)}, u32[]{:S(2)}, u32[]{:S(2)}) %collective-permute-start.18) | collective-permute-done | bytes 262176 | tf_op jit(solution)/shard_map/ppermute | solution.py:33
  82.2 3.3 %collective-permute-done.19 = bf16[64,2048]{1,0:T(8,128)(2,1)S(1)} collective-permute-done((bf16[64,2048]{1,0:T(8,128)(2,1)S(1)}, bf16[64,2048]{1,0:T(8,128)(2,1)S(1)}, u32[]{:S(2)}, u32[]{:S(2)}) %collective-permute-start.19) | collective-permute-done | bytes 262176 | tf_op jit(solution)/shard_map/ppermute | solution.py:33
  85.7 5.5 %collective-permute-done.20 = bf16[64,2048]{1,0:T(8,128)(2,1)S(1)} collective-permute-done((bf16[64,2048]{1,0:T(8,128)(2,1)S(1)}, bf16[64,2048]{1,0:T(8,128)(2,1)S(1)}, u32[]{:S(2)}, u32[]{:S(2)}) %collective-permute-start.20) | collective-permute-done | bytes 262176 | tf_op jit(solution)/shard_map/ppermute | solution.py:33
  93.5 3.3 %collective-permute-done.21 = bf16[64,2048]{1,0:T(8,128)(2,1)S(1)} collective-permute-done((bf16[64,2048]{1,0:T(8,128)(2,1)S(1)}, bf16[64,2048]{1,0:T(8,128)(2,1)S(1)}, u32[]{:S(2)}, u32[]{:S(2)}) %collective-permute-start.21) | collective-permute-done | bytes 262176 | tf_op jit(solution)/shard_map/ppermute | solution.py:33
  96.9 5.0 %collective-permute-done.22 = bf16[64,2048]{1,0:T(8,128)(2,1)S(1)} collective-permute-done((bf16[64,2048]{1,0:T(8,128)(2,1)S(1)}, bf16[64,2048]{1,0:T(8,128)(2,1)S(1)}, u32[]{:S(2)}, u32[]{:S(2)}) %collective-permute-start.22) | collective-permute-done | bytes 262176 | tf_op jit(solution)/shard_map/ppermute | solution.py:33
  104.1 10.7 %collective-permute-done.26.refs_1_ = bf16[64,2048]{1,0:T(8,128)(2,1)S(1)} collective-permute-done((bf16[64,2048]{1,0:T(8,128)(2,1)S(1)}, bf16[64,2048]{1,0:T(8,128)(2,1)S(1)}, u32[]{:S(2)}, u32[]{:S(2)}) %collective-permute-start.26) | collective-permute-done | bytes 262176 | tf_op jit(solution)/shard_map/ppermute | solution.py:43
  114.8 4.2 %collective-permute-done.23.weight.refs_0_ = bf16[64,2048]{1,0:T(8,128)(2,1)S(1)} collective-permute-done((bf16[64,2048]{1,0:T(8,128)(2,1)S(1)}, bf16[64,2048]{1,0:T(8,128)(2,1)S(1)}, u32[]{:S(2)}, u32[]{:S(2)}) %collective-permute-start.23) | collective-permute-done | bytes 262176 | tf_op jit(solution)/shard_map/ppermute | solution.py:43
  122.0 8.0 %collective-permute-done.27.refs_1_ = bf16[64,2048]{1,0:T(8,128)(2,1)S(1)} collective-permute-done((bf16[64,2048]{1,0:T(8,128)(2,1)S(1)}, bf16[64,2048]{1,0:T(8,128)(2,1)S(1)}, u32[]{:S(2)}, u32[]{:S(2)}) %collective-permute-start.27) | collective-permute-done | bytes 262176 | tf_op jit(solution)/shard_map/ppermute | solution.py:33
  132.5 3.1 %collective-permute-done.24.weight.refs_0_ = bf16[64,2048]{1,0:T(8,128)(2,1)S(1)} collective-permute-done((bf16[64,2048]{1,0:T(8,128)(2,1)S(1)}, bf16[64,2048]{1,0:T(8,128)(2,1)S(1)}, u32[]{:S(2)}, u32[]{:S(2)}) %collective-permute-start.24) | collective-permute-done | bytes 262176 | tf_op jit(solution)/shard_map/ppermute | solution.py:33
  135.6 5.0 %collective-permute-done.28.refs_1_ = bf16[64,2048]{1,0:T(8,128)(2,1)S(1)} collective-permute-done((bf16[64,2048]{1,0:T(8,128)(2,1)S(1)}, bf16[64,2048]{1,0:T(8,128)(2,1)S(1)}, u32[]{:S(2)}, u32[]{:S(2)}) %collective-permute-start.28) | collective-permute-done | bytes 262176 | tf_op jit(solution)/shard_map/ppermute | solution.py:33
  154.0 5.1 %mix.3 = (bf16[256,512]{1,0:T(8,128)(2,1)S(1)}, bf16[256,512]{1,0:T(8,128)(2,1)S(1)}, f32[256,128]{1,0:T(8,128)S(1)}, f32[256,128]{1,0:T(8,128)S(1)}) custom-call(s32[2]{0:T(128)S(1)} %pad_add_fusion.where, bf16[512,1024]{1,0:T(8,128)(2,1)S(1)} %get-tuple-element.112.xz_ref, bf16[512,256]{1,0:T(8,128)(2,1)S(1)} %get-tuple-element.113.p_ref, ...), custom_call_target="tpu_custom_call" | custom-call | flops 536870912 | bytes 1835008 | tf_op jit(solution)/shard_map/mix/pallas_call | solution.py:333
  166.0 7.3 %collective-permute-done.41 = bf16[64,2048]{1,0:T(8,128)(2,1)S(1)} collective-permute-done((bf16[64,2048]{1,0:T(8,128)(2,1)S(1)}, bf16[64,2048]{1,0:T(8,128)(2,1)S(1)}, u32[]{:S(2)}, u32[]{:S(2)}) %collective-permute-start.41) | collective-permute-done | bytes 262176 | tf_op jit(solution)/shard_map/ppermute | solution.py:33
  173.4 5.5 %collective-permute-done.42 = bf16[64,2048]{1,0:T(8,128)(2,1)S(1)} collective-permute-done((bf16[64,2048]{1,0:T(8,128)(2,1)S(1)}, bf16[64,2048]{1,0:T(8,128)(2,1)S(1)}, u32[]{:S(2)}, u32[]{:S(2)}) %collective-permute-start.42) | collective-permute-done | bytes 262176 | tf_op jit(solution)/shard_map/ppermute | solution.py:33
  181.1 3.4 %collective-permute-done.43 = bf16[64,2048]{1,0:T(8,128)(2,1)S(1)} collective-permute-done((bf16[64,2048]{1,0:T(8,128)(2,1)S(1)}, bf16[64,2048]{1,0:T(8,128)(2,1)S(1)}, u32[]{:S(2)}, u32[]{:S(2)}) %collective-permute-start.43) | collective-permute-done | bytes 262176 | tf_op jit(solution)/shard_map/ppermute | solution.py:33
  184.6 5.5 %collective-permute-done.44 = bf16[64,2048]{1,0:T(8,128)(2,1)S(1)} collective-permute-done((bf16[64,2048]{1,0:T(8,128)(2,1)S(1)}, bf16[64,2048]{1,0:T(8,128)(2,1)S(1)}, u32[]{:S(2)}, u32[]{:S(2)}) %collective-permute-start.44) | collective-permute-done | bytes 262176 | tf_op jit(solution)/shard_map/ppermute | solution.py:33
  192.4 3.4 %collective-permute-done.45 = bf16[64,2048]{1,0:T(8,128)(2,1)S(1)} collective-permute-done((bf16[64,2048]{1,0:T(8,128)(2,1)S(1)}, bf16[64,2048]{1,0:T(8,128)(2,1)S(1)}, u32[]{:S(2)}, u32[]{:S(2)}) %collective-permute-start.45) | collective-permute-done | bytes 262176 | tf_op jit(solution)/shard_map/ppermute | solution.py:33
  195.8 4.7 %collective-permute-done.46 = bf16[64,2048]{1,0:T(8,128)(2,1)S(1)} collective-permute-done((bf16[64,2048]{1,0:T(8,128)(2,1)S(1)}, bf16[64,2048]{1,0:T(8,128)(2,1)S(1)}, u32[]{:S(2)}, u32[]{:S(2)}) %collective-permute-start.46) | collective-permute-done | bytes 262176 | tf_op jit(solution)/shard_map/ppermute | solution.py:33
  (175 shorter events, 83.9 us)
Async XLA Ops:
  0.0 57.5 %collective-permute-start.15 = (bf16[512,4096]{1,0:T(8,128)(2,1)}, bf16[512,4096]{1,0:T(8,128)(2,1)}, u32[]{:S(2)}, u32[]{:S(2)}) collective-permute-start(bf16[512,4096]{1,0:T(8,128)(2,1)} %bitcast.39), channel_id=1, source_target_pairs={{0,1},{1,0},{2,3},{3,2},{4,5},{5,4},{6,7},{7,6},{8,9},{9,8},{10,11... | collective-permute-start | bytes 12582920 | tf_op jit(solution)/shard_map/ppermute | solution.py:28
  1.6 11.6 %collective-permute-start = (bf16[64,2048]{1,0:T(8,128)(2,1)S(1)}, bf16[64,2048]{1,0:T(8,128)(2,1)S(1)}, u32[]{:S(2)}, u32[]{:S(2)}) collective-permute-start(bf16[64,2048]{1,0:T(8,128)(2,1)S(1)} %get-tuple-element.134.refs_0_), channel_id=1, source_target_pairs={{0,2},{1,3},{2,4},{3,5},{4,6},{5,7},{6,0},{7,1},{8,10},{9,11},{10,... | collective-permute-start | bytes 786440 | tf_op jit(solution)/shard_map/ppermute | solution.py:33
  7.9 12.1 %collective-permute-start.4 = (bf16[64,2048]{1,0:T(8,128)(2,1)S(1)}, bf16[64,2048]{1,0:T(8,128)(2,1)S(1)}, u32[]{:S(2)}, u32[]{:S(2)}) collective-permute-start(bf16[64,2048]{1,0:T(8,128)(2,1)S(1)} %get-tuple-element.68.refs_1_), channel_id=1, source_target_pairs={{0,2},{1,3},{2,4},{3,5},{4,6},{5,7},{6,0},{7,1},{8,10},{9,11},{10,... | collective-permute-start | bytes 786440 | tf_op jit(solution)/shard_map/ppermute | solution.py:33
  13.3 12.1 %collective-permute-start.11 = (bf16[64,2048]{1,0:T(8,128)(2,1)S(1)}, bf16[64,2048]{1,0:T(8,128)(2,1)S(1)}, u32[]{:S(2)}, u32[]{:S(2)}) collective-permute-start(bf16[64,2048]{1,0:T(8,128)(2,1)S(1)} %collective-permute-done.refs_0_), channel_id=1, source_target_pairs={{0,1},{1,0},{2,3},{3,2},{4,5},{5,4},{6,7},{7,6},{8,9},{9,8},{10,11... | collective-permute-start | bytes 786440 | tf_op jit(solution)/shard_map/ppermute | solution.py:28
  13.3 12.0 %collective-permute-start.1 = (bf16[64,2048]{1,0:T(8,128)(2,1)S(1)}, bf16[64,2048]{1,0:T(8,128)(2,1)}, u32[]{:S(2)}, u32[]{:S(2)}) collective-permute-start(bf16[64,2048]{1,0:T(8,128)(2,1)S(1)} %collective-permute-done.refs_0_), channel_id=1, source_target_pairs={{0,2},{1,3},{2,4},{3,5},{4,6},{5,7},{6,0},{7,1},{8,10},{9,11},{10,... | collective-permute-start | bytes 786440 | tf_op jit(solution)/shard_map/ppermute | solution.py:33
  25.3 21.5 %collective-permute-start.9 = (bf16[64,2048]{1,0:T(8,128)(2,1)}, bf16[64,2048]{1,0:T(8,128)(2,1)S(1)}, u32[]{:S(2)}, u32[]{:S(2)}) collective-permute-start(bf16[64,2048]{1,0:T(8,128)(2,1)} %collective-permute-done.1.refs_0_), channel_id=1, source_target_pairs={{0,1},{1,0},{2,3},{3,2},{4,5},{5,4},{6,7},{7,6},{8,9},{9,8},{10,11... | collective-permute-start | bytes 786440 | tf_op jit(solution)/shard_map/ppermute | solution.py:28
  26.0 11.7 %collective-permute-start.2 = (bf16[64,2048]{1,0:T(8,128)(2,1)}, bf16[64,2048]{1,0:T(8,128)(2,1)S(1)}, u32[]{:S(2)}, u32[]{:S(2)}) collective-permute-start(bf16[64,2048]{1,0:T(8,128)(2,1)} %collective-permute-done.1.refs_0_), channel_id=1, source_target_pairs={{0,2},{1,3},{2,4},{3,5},{4,6},{5,7},{6,0},{7,1},{8,10},{9,11},{10,... | collective-permute-start | bytes 786440 | tf_op jit(solution)/shard_map/ppermute | solution.py:33
  30.8 16.1 %collective-permute-start.10 = (bf16[64,2048]{1,0:T(8,128)(2,1)}, bf16[64,2048]{1,0:T(8,128)(2,1)S(1)}, u32[]{:S(2)}, u32[]{:S(2)}) collective-permute-start(bf16[64,2048]{1,0:T(8,128)(2,1)} %collective-permute-done.5.refs_1_), channel_id=1, source_target_pairs={{0,1},{1,0},{2,3},{3,2},{4,5},{5,4},{6,7},{7,6},{8,9},{9,8},{10,11... | collective-permute-start | bytes 786440 | tf_op jit(solution)/shard_map/ppermute | solution.py:28
  37.7 11.8 %collective-permute-start.7 = (bf16[64,2048]{1,0:T(8,128)(2,1)S(1)}, bf16[64,2048]{1,0:T(8,128)(2,1)S(1)}, u32[]{:S(2)}, u32[]{:S(2)}) collective-permute-start(bf16[64,2048]{1,0:T(8,128)(2,1)S(1)} %collective-permute-done.2.refs_0_), channel_id=1, source_target_pairs={{0,1},{1,0},{2,3},{3,2},{4,5},{5,4},{6,7},{7,6},{8,9},{9,8},{10,11... | collective-permute-start | bytes 786440 | tf_op jit(solution)/shard_map/ppermute | solution.py:28
  68.1 11.8 %collective-permute-start.18 = (bf16[64,2048]{1,0:T(8,128)(2,1)S(1)}, bf16[64,2048]{1,0:T(8,128)(2,1)S(1)}, u32[]{:S(2)}, u32[]{:S(2)}) collective-permute-start(bf16[64,2048]{1,0:T(8,128)(2,1)S(1)} %out_project.11), channel_id=1, source_target_pairs={{0,2},{1,3},{2,4},{3,5},{4,6},{5,7},{6,0},{7,1},{8,10},{9,11},{10,... | collective-permute-start | bytes 786440 | tf_op jit(solution)/shard_map/ppermute | solution.py:33
  74.4 11.2 %collective-permute-start.19 = (bf16[64,2048]{1,0:T(8,128)(2,1)S(1)}, bf16[64,2048]{1,0:T(8,128)(2,1)S(1)}, u32[]{:S(2)}, u32[]{:S(2)}) collective-permute-start(bf16[64,2048]{1,0:T(8,128)(2,1)S(1)} %convert_add_fusion.7), channel_id=1, source_target_pairs={{0,2},{1,3},{2,4},{3,5},{4,6},{5,7},{6,0},{7,1},{8,10},{9,11},{10,... | collective-permute-start | bytes 786440 | tf_op jit(solution)/shard_map/ppermute | solution.py:33
  80.0 11.2 %collective-permute-start.20 = (bf16[64,2048]{1,0:T(8,128)(2,1)S(1)}, bf16[64,2048]{1,0:T(8,128)(2,1)S(1)}, u32[]{:S(2)}, u32[]{:S(2)}) collective-permute-start(bf16[64,2048]{1,0:T(8,128)(2,1)S(1)} %add_convert_fusion.3), channel_id=1, source_target_pairs={{0,2},{1,3},{2,4},{3,5},{4,6},{5,7},{6,0},{7,1},{8,10},{9,11},{10,... | collective-permute-start | bytes 786440 | tf_op jit(solution)/shard_map/ppermute | solution.py:33
  85.6 11.2 %collective-permute-start.21 = (bf16[64,2048]{1,0:T(8,128)(2,1)S(1)}, bf16[64,2048]{1,0:T(8,128)(2,1)S(1)}, u32[]{:S(2)}, u32[]{:S(2)}) collective-permute-start(bf16[64,2048]{1,0:T(8,128)(2,1)S(1)} %convert_add_fusion.6), channel_id=1, source_target_pairs={{0,2},{1,3},{2,4},{3,5},{4,6},{5,7},{6,0},{7,1},{8,10},{9,11},{10,... | collective-permute-start | bytes 786440 | tf_op jit(solution)/shard_map/ppermute | solution.py:33
  102.0 12.8 %collective-permute-start.26 = (bf16[64,2048]{1,0:T(8,128)(2,1)S(1)}, bf16[64,2048]{1,0:T(8,128)(2,1)S(1)}, u32[]{:S(2)}, u32[]{:S(2)}) collective-permute-start(bf16[64,2048]{1,0:T(8,128)(2,1)S(1)} %slice_select_fusion), channel_id=1, source_target_pairs={{0,10},{1,11},{2,12},{3,13},{4,14},{5,15},{6,8},{7,9},{8,18},{9,19... | collective-permute-start | bytes 786440 | tf_op jit(solution)/shard_map/ppermute | solution.py:43
  102.0 17.0 %collective-permute-start.23 = (bf16[64,2048]{1,0:T(8,128)(2,1)S(1)}, bf16[64,2048]{1,0:T(8,128)(2,1)S(1)}, u32[]{:S(2)}, u32[]{:S(2)}) collective-permute-start(bf16[64,2048]{1,0:T(8,128)(2,1)S(1)} %get-tuple-element.104.weight), channel_id=1, source_target_pairs={{0,10},{1,11},{2,12},{3,13},{4,14},{5,15},{6,8},{7,9},{8,18},{9,19... | collective-permute-start | bytes 786440 | tf_op jit(solution)/shard_map/ppermute | solution.py:43
  119.6 12.9 %collective-permute-start.36 = (bf16[64,2048]{1,0:T(8,128)(2,1)S(1)}, bf16[64,2048]{1,0:T(8,128)(2,1)S(1)}, u32[]{:S(2)}, u32[]{:S(2)}) collective-permute-start(bf16[64,2048]{1,0:T(8,128)(2,1)S(1)} %slice_select_fusion), channel_id=1, source_target_pairs={{0,8},{1,9},{2,10},{3,11},{4,12},{5,13},{6,14},{7,15},{8,16},{9,17... | collective-permute-start | bytes 786440 | tf_op jit(solution)/shard_map/ppermute | solution.py:43
  122.0 13.7 %collective-permute-start.24 = (bf16[64,2048]{1,0:T(8,128)(2,1)S(1)}, bf16[64,2048]{1,0:T(8,128)(2,1)S(1)}, u32[]{:S(2)}, u32[]{:S(2)}) collective-permute-start(bf16[64,2048]{1,0:T(8,128)(2,1)S(1)} %collective-permute-done.23.weight.refs_0_), channel_id=1, source_target_pairs={{0,2},{1,3},{2,4},{3,5},{4,6},{5,7},{6,0},{7,1},{8,10},{9,11},{10,... | collective-permute-start | bytes 786440 | tf_op jit(solution)/shard_map/ppermute | solution.py:33
  122.0 13.7 %collective-permute-start.34 = (bf16[64,2048]{1,0:T(8,128)(2,1)S(1)}, bf16[64,2048]{1,0:T(8,128)(2,1)S(1)}, u32[]{:S(2)}, u32[]{:S(2)}) collective-permute-start(bf16[64,2048]{1,0:T(8,128)(2,1)S(1)} %collective-permute-done.26.refs_1_), channel_id=1, source_target_pairs={{0,1},{1,0},{2,3},{3,2},{4,5},{5,4},{6,7},{7,6},{8,9},{9,8},{10,11... | collective-permute-start | bytes 786440 | tf_op jit(solution)/shard_map/ppermute | solution.py:28
  132.5 12.1 %collective-permute-start.38 = (bf16[64,2048]{1,0:T(8,128)(2,1)S(1)}, bf16[64,2048]{1,0:T(8,128)(2,1)S(1)}, u32[]{:S(2)}, u32[]{:S(2)}) collective-permute-start(bf16[64,2048]{1,0:T(8,128)(2,1)S(1)} %collective-permute-done.36.refs_1_), channel_id=1, source_target_pairs={{0,1},{1,0},{2,3},{3,2},{4,5},{5,4},{6,7},{7,6},{8,9},{9,8},{10,11... | collective-permute-start | bytes 786440 | tf_op jit(solution)/shard_map/ppermute | solution.py:28
  135.6 11.7 %collective-permute-start.33 = (bf16[64,2048]{1,0:T(8,128)(2,1)S(1)}, bf16[64,2048]{1,0:T(8,128)(2,1)S(1)}, u32[]{:S(2)}, u32[]{:S(2)}) collective-permute-start(bf16[64,2048]{1,0:T(8,128)(2,1)S(1)} %collective-permute-done.23.weight.refs_0_), channel_id=1, source_target_pairs={{0,1},{1,0},{2,3},{3,2},{4,5},{5,4},{6,7},{7,6},{8,9},{9,8},{10,11... | collective-permute-start | bytes 786440 | tf_op jit(solution)/shard_map/ppermute | solution.py:28
  163.8 15.1 %collective-permute-start.42 = (bf16[64,2048]{1,0:T(8,128)(2,1)S(1)}, bf16[64,2048]{1,0:T(8,128)(2,1)S(1)}, u32[]{:S(2)}, u32[]{:S(2)}) collective-permute-start(bf16[64,2048]{1,0:T(8,128)(2,1)S(1)} %out_project.16), channel_id=1, source_target_pairs={{0,2},{1,3},{2,4},{3,5},{4,6},{5,7},{6,0},{7,1},{8,10},{9,11},{10,... | collective-permute-start | bytes 786440 | tf_op jit(solution)/shard_map/ppermute | solution.py:33
  173.4 11.2 %collective-permute-start.43 = (bf16[64,2048]{1,0:T(8,128)(2,1)S(1)}, bf16[64,2048]{1,0:T(8,128)(2,1)S(1)}, u32[]{:S(2)}, u32[]{:S(2)}) collective-permute-start(bf16[64,2048]{1,0:T(8,128)(2,1)S(1)} %convert_add_fusion.3), channel_id=1, source_target_pairs={{0,2},{1,3},{2,4},{3,5},{4,6},{5,7},{6,0},{7,1},{8,10},{9,11},{10,... | collective-permute-start | bytes 786440 | tf_op jit(solution)/shard_map/ppermute | solution.py:33
  179.0 11.2 %collective-permute-start.44 = (bf16[64,2048]{1,0:T(8,128)(2,1)S(1)}, bf16[64,2048]{1,0:T(8,128)(2,1)S(1)}, u32[]{:S(2)}, u32[]{:S(2)}) collective-permute-start(bf16[64,2048]{1,0:T(8,128)(2,1)S(1)} %add_convert_fusion.1), channel_id=1, source_target_pairs={{0,2},{1,3},{2,4},{3,5},{4,6},{5,7},{6,0},{7,1},{8,10},{9,11},{10,... | collective-permute-start | bytes 786440 | tf_op jit(solution)/shard_map/ppermute | solution.py:33
  184.6 11.2 %collective-permute-start.45 = (bf16[64,2048]{1,0:T(8,128)(2,1)S(1)}, bf16[64,2048]{1,0:T(8,128)(2,1)S(1)}, u32[]{:S(2)}, u32[]{:S(2)}) collective-permute-start(bf16[64,2048]{1,0:T(8,128)(2,1)S(1)} %convert_add_fusion.2), channel_id=1, source_target_pairs={{0,2},{1,3},{2,4},{3,5},{4,6},{5,7},{6,0},{7,1},{8,10},{9,11},{10,... | collective-permute-start | bytes 786440 | tf_op jit(solution)/shard_map/ppermute | solution.py:33
  (49 other events, 422.2 us)
